TPU v7x, 256 devices: a whole 4x4x8 slice. The times are simulated.
256 devices in a mesh: section: 4 (over y), chan: 64 (over x, z, core).
Axes of the slice: x: 4, y: 4, z: 8, core: 2. Of those that a mesh axis runs over, the one named last changes fastest.
Arguments:
- voltages: bfloat16 [2, 1024, 16, 4096], P(None, 'chan', 'section'), may hold values from -6 to 6
- coefficients: float32 [4, 4096], replicated, may hold values from -0.046875 to 0.046875
- tile_order: int32 [64, 36], P('chan'), may hold values from 0 to 35, each once within a row
- steer_table: bfloat16 [256, 2, 512], replicated, may hold values from -0.1875 to 0.1875
- beam_index: int32 [256, 64], P(None, 'chan'), may hold values from 0 to 255
Outputs:
- visibility: float32 [64, 36, 2, 128, 128], P('chan', 'section')
- beam_power: float32 [2, 256, 16, 4096], P(None, None, 'section', 'chan')
Inputs may be any that keep to these rules, and one draw needn't show every extreme that they name: Row g of tile_order lists each of the 36 work items of channel column g exactly once.
All inputs are finite; a program needn't handle non-finite values.
Results may differ from a plain program's by a relative error of at most 0.0029.
Values may be sent and summed in bfloat16 or wider, within the bound.
A program may use at most 64 MiB of HBM per device.

v0:
```python
import math

import jax
import jax.numpy as jnp
from jax import lax
from jax.sharding import PartitionSpec as P

STATIONS = 512
INPUTS = 1024
NA = 64
NB = 64
AVG = 64
TB = 128
PAIRS = 36
NBEAM = 256


def shifted(value, axis, by):
    devices = lax.axis_size(axis)
    pairs = [(i, i + by) for i in range(devices) if 0 <= i + by < devices]
    return lax.ppermute(value, axis, pairs)


def dft_table(length):
    counter = lax.iota(jnp.int32, length)
    phases = counter[:, None] * counter[None, :] % length
    angles = 2.0 * math.pi / length * phases.astype(jnp.float32)
    cosine = jnp.cos(angles)
    sine_part = jnp.sin(angles)
    return jnp.stack([jnp.stack([cosine, -sine_part]), jnp.stack([sine_part, cosine])])


def channelize(filtered):
    spectra_count = filtered.shape[1]
    length = NA * NB
    blocks = filtered.reshape(2, spectra_count, NA, NB)
    section_one = jnp.einsum("qmab,qrac->rmcb", blocks, dft_table(NA), precision=lax.Precision.HIGH)
    row_index = lax.iota(jnp.int32, NA)
    col_index = lax.iota(jnp.int32, NB)
    angles = (
        2.0
        * math.pi
        / length
        * (row_index[:, None] * col_index[None, :] % length).astype(jnp.float32)
    )
    cosine = jnp.cos(angles)
    sine_part = jnp.sin(angles)
    turned_real = section_one[0] * cosine + section_one[1] * sine_part
    turned_imag = section_one[1] * cosine - section_one[0] * sine_part
    twisted = jnp.stack([turned_real, turned_imag])
    section_two = jnp.einsum(
        "rmcb,rsbd->smdc", twisted, dft_table(NB), precision=lax.Precision.HIGH
    )
    return section_two.reshape(2, spectra_count, length)


def pair_products(spectra, work_items):
    tile_count = INPUTS // TB
    local_channel = work_items // PAIRS
    pair_number = work_items % PAIRS
    tile_ids = lax.iota(jnp.int32, tile_count)
    first_pairs = tile_ids * (tile_ids + 1) // 2
    row_tiles = (
        jnp.sum((first_pairs[None, :] <= pair_number[:, None]).astype(jnp.int32), axis=1) - 1
    )
    col_tiles = pair_number - row_tiles * (row_tiles + 1) // 2
    frame_count = spectra.shape[2]
    channel_groups = spectra.shape[3] // AVG
    blocks = spectra.reshape(2, tile_count, TB, frame_count, channel_groups, AVG)
    tile_table = jnp.transpose(blocks, (1, 4, 0, 2, 3, 5)).reshape(
        tile_count * channel_groups, 2, TB, frame_count * AVG
    )
    row_block = jnp.take(tile_table, row_tiles * channel_groups + local_channel, axis=0)
    col_block = jnp.take(tile_table, col_tiles * channel_groups + local_channel, axis=0)
    swapped = jnp.stack([row_block[:, 1], -row_block[:, 0]], axis=1)
    numbers = (((1, 3), (1, 3)), ((0,), (0,)))
    real_part = lax.dot_general(row_block, col_block, numbers, preferred_element_type=jnp.float32)
    imag_part = lax.dot_general(swapped, col_block, numbers, preferred_element_type=jnp.float32)
    return jnp.stack([real_part, imag_part], axis=1)


def shards(voltages, coefficients, tile_order, steer_table, beam_index):
    section_count = lax.axis_size("section")
    inputs_dev = voltages.shape[1]
    frames_dev = voltages.shape[2]
    tap_count = coefficients.shape[0]
    history = shifted(voltages[:, :, frames_dev - (tap_count - 1) :, :], "section", 1)
    extended = jnp.concatenate([history, voltages], axis=2).astype(jnp.float32)
    filtered = jnp.zeros(voltages.shape, jnp.float32)
    for tap_index in range(tap_count):
        offset = tap_count - 1 - tap_index
        filtered = (
            filtered + coefficients[tap_index] * extended[:, :, offset : offset + frames_dev, :]
        )
    spectra = (
        channelize(filtered.reshape(2, inputs_dev * frames_dev, NA * NB))
        .reshape(voltages.shape)
        .astype(jnp.bfloat16)
    )
    weights = steer_table[beam_index]
    out_dev = beam_index.shape[1]
    shard_piece = lax.all_to_all(spectra, "chan", split_axis=3, concat_axis=1, tiled=True)
    frame_count = shard_piece.shape[2]
    grouped = shard_piece.reshape(2, STATIONS, 2, frame_count, out_dev, AVG)
    product = lax.dot_general(
        weights, grouped, (((3,), (1,)), ((1,), (4,))), preferred_element_type=jnp.float32
    )
    real_part = product[:, :, 0, 0] - product[:, :, 1, 1]
    imag_part = product[:, :, 0, 1] + product[:, :, 1, 0]
    beam_energy = real_part * real_part + imag_part * imag_part
    beam_power = jnp.transpose(beam_energy, (2, 1, 3, 0, 4)).reshape(
        2, NBEAM, frame_count, out_dev * AVG
    )
    column_items = tile_order[0]
    items_dev = column_items.shape[0] // section_count
    mean_factor = 1.0 / (frames_dev * section_count * AVG)
    own_items = lax.dynamic_slice_in_dim(
        column_items, lax.axis_index("section") * items_dev, items_dev
    )
    totals = pair_products(lax.all_gather(shard_piece, "section", axis=2, tiled=True), own_items)
    visibility = (totals * mean_factor)[None]
    return (visibility, beam_power)


def solution(mesh):
    placed = (P(None, "chan", "section", None), P(), P("chan", None), P(), P(None, "chan"))
    return jax.shard_map(
        shards,
        mesh=mesh,
        in_specs=placed,
        out_specs=(P("chan", "section", None, None, None), P(None, None, "section", "chan")),
        check_vma=False,
    )
```

profile of v0, /device:TPU:1, one launch (start us, length us, event | category | flops | bytes accessed | tf_op | source)
XLA Modules:
  0.0 257.8 jit_solution(14299678543089905093)
XLA Ops:
  7.2 1.9 slice.54
  9.7 4.1 %collective-permute-start = (bf16[2,16,3,4096]{3,1,2,0:T(8,128)(2,1)S(1)}, bf16[2,16,3,4096]{3,1,2,0:T(8,128)(2,1)S(1)}, u32[]{:S(2)}, u32[]{:S(2)}) collective-permute-start(bf16[2,16,3,4096]{3,1,2,0:T(8,128)(2,1)S(1)} %copy.79), channel_id=1, source_target_pairs={{0,64},{64,128},{128,192},{1,65},{65,129},{129,193},{2,66},{66,130... | collective-permute-start | bytes 2359304 | tf_op jit(solution)/shard_map/ppermute | solution.py:21
  14.4 15.6 %collective-permute-done = bf16[2,16,3,4096]{3,1,2,0:T(8,128)(2,1)S(1)} collective-permute-done((bf16[2,16,3,4096]{3,1,2,0:T(8,128)(2,1)S(1)}, bf16[2,16,3,4096]{3,1,2,0:T(8,128)(2,1)S(1)}, u32[]{:S(2)}, u32[]{:S(2)}) %collective-permute-start) | collective-permute-done | bytes 786464 | tf_op jit(solution)/shard_map/ppermute | solution.py:21
  31.7 1.8 fusion.14
  33.5 3.3 %reshape_reshape.4 = f32[2,64,64,64]{3,2,1,0:T(8,128)} reshape(f32[2,16,4,4096]{3,2,1,0:T(4,128)S(1)} %fusion.14) | data formatting | bytes 4194304 | tf_op jit(solution)/shard_map/reshape;reshape | solution.py:36
  36.9 4.2 %fusion.10 = f32[2,64,64,64]{3,2,1,0:T(8,128)S(1)} fusion(f32[2,64,64,64]{3,2,1,0:T(8,128)} %reshape_reshape.4, f32[1,2,64,64]{2,3,0,1:T(8,128)S(1)} %get-tuple-element.27, f32[1,2,64,64]{2,3,0,1:T(8,128)S(1)} %get-tuple-element.26), kind=kOutput, calls=%fused_computation.18 | convolution fusion | flops 402669568 | bytes 4259840 | tf_op jit(solution)/shard_map/qmab,qrac->rmcb/dot_general | solution.py:37
  42.0 3.3 %fusion.13 = bf16[2,64,64,64]{3,2,1,0:T(8,128)(2,1)S(1)} fusion(f32[1,2,64,64]{2,3,0,1:T(8,128)S(1)} %get-tuple-element.27, f32[1,2,64,64]{2,3,0,1:T(8,128)S(1)} %get-tuple-element.26, f32[1,64,64,64]{3,2,1,0:T(8,128)S(1)} %get-tuple-element.21, f32[1,64,64,64]{3,2,1,0:T(8,128)S(1)} %get-tuple-element.20), kind=kOutput, calls=%fused_computation.19 | convolution fusion | flops 403718144 | bytes 3211264 | tf_op jit(solution)/shard_map/rmcb,rsbd->smdc/dot_general | solution.py:51
  45.3 2.2 convert_element_type.61
  47.5 12.0 %copy.55 = bf16[2,16,4,4096]{1,2,0,3:T(4,128)(2,1)} copy(bf16[2,16,4,4096]{3,2,1,0:T(4,128)(2,1)} %convert_element_type.61) | data formatting | bytes 2097152 | tf_op jit(solution)/shard_map/convert_element_type | solution.py:98
  59.5 11.9 %reshape.317 = bf16[64,2,4096]{2,1,0:T(2,128)(2,1)S(1)} reshape(bf16[4096,2,4,16]{3,2,1,0:T(4,128)(2,1)} %bitcast.95) | data formatting | bytes 2097152
  71.4 41.3 %all_to_all.18 = bf16[64,2,4096]{2,1,0:T(2,128)(2,1)S(1)} all-to-all(bf16[64,2,4096]{2,1,0:T(2,128)(2,1)S(1)} %reshape.317), channel_id=1, replica_groups=mesh['section'=4,'chan'=64] {'chan'}, dimensions={0} | all-to-all | bytes 2097152 | tf_op jit(solution)/shard_map/all_to_all | solution.py:102
  112.7 7.5 %reshape.318 = bf16[4096,2,4,16]{3,2,1,0:T(4,128)(2,1)} reshape(bf16[64,2,4096]{2,1,0:T(2,128)(2,1)S(1)} %all_to_all.18) | data formatting | bytes 2097152
  120.3 11.4 %copy.75 = bf16[2,16,4,64,64]{4,1,3,2,0:T(8,128)(2,1)} copy(bf16[2,16,4,64,64]{1,2,0,4,3:T(4,128)(2,1)} %bitcast.94) | data formatting | bytes 2097152 | tf_op jit(solution)/shard_map/all_to_all | solution.py:102
  131.7 1.7 gather_fusion
  133.9 3.5 %copy.64 = bf16[2,512,2,4,64]{1,4,3,2,0:T(8,128)(2,1)} copy(bf16[2,512,2,4,64]{4,2,1,3,0:T(2,128)(2,1)S(1)} %bitcast.97) | data formatting | bytes 2097152 | tf_op jit(solution)/shard_map/reshape.8
  137.4 2.0 convolution_bitcast_fusion
  140.3 74.9 %all-gather.2.cloned.1.call-done = bf16[2,1024,16,64]{3,1,2,0:T(8,128)(2,1)} async-done(((bf16[2,1024,4,64]{3,1,2,0:T(8,128)(2,1)}), bf16[2,1024,16,64]{3,1,2,0:T(8,128)(2,1)}) %all-gather.2.cloned.1.call-update) | async-done | bytes 4194320 | tf_op jit(solution)/shard_map/all_gather | solution.py:120
  215.2 8.6 %copy.58 = bf16[2,8,128,16,1,64]{2,5,3,0,1,4:T(8,128)(2,1)} copy(bf16[2,8,128,16,1,64]{5,2,1,3,0,4:T(8,128)(2,1)} %bitcast.98) | data formatting | bytes 8388608 | tf_op jit(solution)/shard_map/reshape | solution.py:69
  223.8 6.5 %copy.59 = bf16[8,2,128,1024]{3,2,1,0:T(8,128)(2,1)} copy(bf16[8,2,128,1024]{2,3,1,0:T(8,128)(2,1)} %bitcast.92) | data formatting | bytes 8388608 | tf_op jit(solution)/shard_map/reshape | solution.py:70
  230.3 5.8 %gather_fusion.2 = bf16[9,2,128,1024]{2,3,1,0:T(8,128)(2,1)} fusion(bf16[8,2,128,1024]{2,3,1,0:T(8,128)(2,1)} %bitcast.93, s32[1024]{0:T(1024)S(1)} %pad_clamp_fusion.1), kind=kCustom, calls=%fused_computation.1.clone | custom fusion | bytes 9437220 | tf_op jit(solution)/shard_map/jit(_take)/gather | solution.py:74
  236.1 5.9 %gather_fusion.1 = bf16[9,2,128,1024]{3,2,1,0:T(8,128)(2,1)} fusion(bf16[8,2,128,1024]{3,2,1,0:T(8,128)(2,1)} %copy.59, s32[1024]{0:T(1024)S(1)} %pad_clamp_fusion.2), kind=kCustom, calls=%fused_computation.clone | custom fusion | bytes 9437220 | tf_op jit(solution)/shard_map/jit(_take)/gather | solution.py:73
  242.0 3.0 %broadcast_select_fusion.1 = bf16[9,2,128,1024]{3,2,1,0:T(8,128)(2,1)S(1)} fusion(bf16[9,2,128,1024]{3,2,1,0:T(8,128)(2,1)} %gather_fusion.1, pred[9]{0:T(512)(128)(4,1)S(1)} %get-tuple-element.13), kind=kLoop, calls=%fused_computation.8 | loop fusion | flops 2359296 | bytes 9437193 | tf_op jit(solution)/shard_map/jit(_take)/select_n | solution.py:73
  246.2 1.4 fusion.20
  247.7 2.0 fusion.21
  (43 shorter events, 7.6 us)
Async XLA Ops:
  7.2 124.6 %copy-start = (bf16[256,2,512]{2,1,0:T(2,128)(2,1)S(1)}, bf16[256,2,512]{2,1,0:T(2,128)(2,1)}, u32[]{:S(2)}) copy-start(bf16[256,2,512]{2,1,0:T(2,128)(2,1)} %param.10) | copy-start | bytes 1572868
  7.2 7.1 %copy-start.4 = (f32[4,4096]{1,0:T(4,128)S(1)}, f32[4,4096]{1,0:T(4,128)}, u32[]{:S(2)}) copy-start(f32[4,4096]{1,0:T(4,128)} %param.8) | copy-start | bytes 196612
  7.2 208.1 %all-gather.2.cloned.1.call-start = ((), (), s32[]{:S(2)}) async-start(), calls=%async_computation.1 | async-start | bytes 10485760 | tf_op jit(solution)/shard_map/all_gather | solution.py:120
  9.1 21.5 %copy-start.3 = (bf16[2,16,4,4096]{3,2,1,0:T(4,128)(2,1)S(1)}, bf16[2,16,4,4096]{3,2,1,0:T(4,128)(2,1)}, u32[]{:S(2)}) copy-start(bf16[2,16,4,4096]{3,2,1,0:T(4,128)(2,1)} %param.7) | copy-start | bytes 3145732
  9.7 20.2 %collective-permute-start = (bf16[2,16,3,4096]{3,1,2,0:T(8,128)(2,1)S(1)}, bf16[2,16,3,4096]{3,1,2,0:T(8,128)(2,1)S(1)}, u32[]{:S(2)}, u32[]{:S(2)}) collective-permute-start(bf16[2,16,3,4096]{3,1,2,0:T(8,128)(2,1)S(1)} %copy.79), channel_id=1, source_target_pairs={{0,64},{64,128},{128,192},{1,65},{65,129},{129,193},{2,66},{66,130... | collective-permute-start | bytes 2359304 | tf_op jit(solution)/shard_map/ppermute | solution.py:21
  120.3 11.4 %copy-start.6 = (s32[256,1]{0,1:T(1,128)S(1)}, s32[256,1]{0,1:T(1,128)}, u32[]{:S(2)}) copy-start(s32[256,1]{0,1:T(1,128)} %param.11) | copy-start | bytes 3076
  131.6 1.8 copy-start.5
  131.6 2.2 copy-start.2
  242.0 3.6 %slice-start = ((s8[4718592]{0:T(1024)(128)(4,1)}), s8[4194304]{0:T(1024)(128)(4,1)S(1)}, s32[]{:S(2)}) async-start(s8[4718592]{0:T(1024)(128)(4,1)} %bitcast.99), calls=%async_computation.2 | async-start | bytes 8388608
  245.0 1.2 slice-start.1
  247.7 3.3 %copy-start.1 = (bf16[256,2,512]{2,1,0:T(2,128)(2,1)S(1)}, bf16[256,2,512]{2,1,0:T(2,128)(2,1)}, u32[]{:S(2)}) copy-start(bf16[256,2,512]{2,1,0:T(2,128)(2,1)} %param.10) | copy-start | bytes 1572868
Sparse Core Ops, SparseCore 0:
  131.8 83.4 all-gather.1
where the time goes:
time: 259 us; the launch traced here: 258 us
  waiting for transfers between devices  90.6 us (35%)
  local copies, waits for them, and re-layouts  85.6 us (33%)
  blocking collectives  41.3 us (16%)
  between operations  14.3 us (6%)
  matrix products  12.9 us (5%)
  other arithmetic  9 us (3%)
  starting transfers between devices  4.11 us (2%)
    all_gather x1, waiting for transfers between devices, shards(): lax.all_gather(shard_piece, 'section', axis=2, tiled=True)  74.9 us
    all_to_all x1, blocking collectives, shards(): lax.all_to_all(spectra, 'chan', split_axis=3, concat_axis=1, tiled=True)  41.3 us
    unnamed x22, local copies, waits for them, and re-layouts  22.1 us
    ppermute x1, waiting for transfers between devices, shifted(): return lax.ppermute(value, axis, pairs)  15.6 us
    convert_element_type x2, local copies, waits for them, and re-layouts, shards(): spectra = channelize(filtered.reshape(2, inputs_dev * frames_dev, NA * NB...  14.2 us
    all_to_all x1, local copies, waits for them, and re-layouts, shards(): lax.all_to_all(spectra, 'chan', split_axis=3, concat_axis=1, tiled=True)  11.4 us
    reshape x1, local copies, waits for them, and re-layouts, pair_products(): spectra.reshape(2, tile_count, TB, frame_count, channel_groups, AVG)  8.56 us
    reshape x1, local copies, waits for them, and re-layouts, pair_products(): jnp.transpose(blocks, (1, 4, 0, 2, 3, 5))  6.46 us
  transfers between devices with their start and end apart: 2, of which 2 were waited for; matrix products, arithmetic and copies ran while one was open for 4% of the time, Pallas kernels for 0%

commit v1 on v0

v1 whole, which is shorter than its diff:
```python
import functools

import jax
import jax.numpy as jnp
import ml_dtypes
import numpy as np
from jax import lax
from jax.experimental import pallas as pl
from jax.experimental.pallas import tpu as pltpu
from jax.sharding import PartitionSpec as P

NSEC = 4
NX, NZ, NCORE = 4, 8, 2
NCHAN = NX * NZ * NCORE
XBLOCK = NZ * NCORE
LOCAL = 16
NCH = 4096
TAPS = 4
NA = 32
NL = 128
AVG = 64
TB = 128
ITEMS = 9
NBEAM = 256
STATIONS = 512
INPUTS = 1024
MEAN = 1.0 / 1024.0
NT = (((1,), (1,)), ((), ()))
NN = (((1,), (0,)), ((), ()))
TN = (((0,), (0,)), ((), ()))
MESH = pl.DeviceIdType.MESH


def split_np(table):
    high = table.astype(ml_dtypes.bfloat16)
    low = (table - high.astype(np.float64)).astype(ml_dtypes.bfloat16)
    return high, low


def tables():
    c = np.arange(NA)
    angle = 2.0 * np.pi / NA * ((c[:, None] * c[None, :]) % NA)
    cosine, sine = np.cos(angle), np.sin(angle)
    first = np.block([[cosine, sine], [-sine, cosine]])
    high, low = split_np(first)
    first = np.concatenate([high, low, high], axis=1)
    channel = np.arange(AVG)
    lane = np.arange(NL)
    angle = 2.0 * np.pi / NCH * ((channel[:, None] * lane[None, :]) % NCH)
    twiddle = np.stack([np.cos(angle), np.sin(angle)]).astype(np.float32)
    group = np.arange(NCHAN)
    angle = 2.0 * np.pi / NCHAN * ((group[:, None] * lane[None, :]) % NCHAN)
    cosine, sine = np.cos(angle), np.sin(angle)
    second = np.stack(
        [np.concatenate([cosine, sine], axis=1), np.concatenate([-sine, cosine], axis=1)], axis=1
    ).reshape(2 * NCHAN, 2 * NL)
    high, low = split_np(second)
    second = np.concatenate([high, low, high], axis=1)
    return jnp.asarray(first), jnp.asarray(twiddle), jnp.asarray(second)


def split(value):
    high = value.astype(jnp.bfloat16)
    return high, (value - high.astype(jnp.float32)).astype(jnp.bfloat16)


def channelize_kernel(own_ref, past_ref, coef_ref, first_ref, twid_ref, second_ref, out_ref, rows_ref):
    for pair in range(2):

        @pl.loop(0, LOCAL)
        def _(i):
            columns = []
            for t2 in range(2):
                t = 2 * pair + t2
                parts = []
                for q in range(2):
                    total = None
                    for p in range(TAPS):
                        source = own_ref[q, i, t - p] if t >= p else past_ref[q, i, t - p + TAPS - 1]
                        term = coef_ref[p] * source.astype(jnp.float32)
                        total = term if total is None else total + term
                    parts.append(total)
                columns.append(jnp.concatenate(parts, axis=0))
            samples = jnp.concatenate(columns, axis=1)
            high, low = split(samples)
            stacked = jnp.concatenate([high, high, low], axis=0)
            section_one = lax.dot_general(
                first_ref[...], stacked, NN, preferred_element_type=jnp.float32
            )
            rows = []
            for t2 in range(2):
                real = section_one[:NA, t2 * NL : (t2 + 1) * NL]
                imag = section_one[NA:, t2 * NL : (t2 + 1) * NL]
                real = jnp.concatenate([real, real], axis=0)
                imag = jnp.concatenate([imag, imag], axis=0)
                cosine, sine = twid_ref[0], twid_ref[1]
                rows.append(
                    jnp.concatenate(
                        [real * cosine + imag * sine, imag * cosine - real * sine], axis=1
                    )
                )
            turned = jnp.concatenate(rows, axis=0)
            high, low = split(turned)
            stacked = jnp.concatenate([high, high, low], axis=1)
            section_two = lax.dot_general(
                second_ref[...], stacked, NT, preferred_element_type=jnp.float32
            )
            rows_ref[pl.ds(i, 2 * NCHAN, stride=LOCAL), :] = section_two

        out_ref[pair] = rows_ref[...].astype(jnp.bfloat16).reshape(NCHAN, 2, LOCAL, NL)


def exchange_kernel(send_ref, all_ref, local_sem, out_sem, in_sem, ysend_sem, yin_sem):
    section = lax.axis_index("section")
    chan = lax.axis_index("chan")
    x, z, core = chan // XBLOCK, (chan % XBLOCK) // NCORE, chan % NCORE
    right, left = (section + 1) % NSEC, (section + NSEC - 1) % NSEC

    def peer_of(dx, j):
        dz, dc = j // NCORE, j % NCORE
        return ((x + dx) % NX) * XBLOCK + ((z + dz) % NZ) * NCORE + (core + dc) % NCORE

    barrier = pltpu.get_barrier_semaphore()

    @pl.loop(1, NCHAN)
    def _(k):
        pl.semaphore_signal(
            barrier, inc=1, device_id=(section, (chan + k) % NCHAN), device_id_type=MESH
        )

    for other in (left, right):
        pl.semaphore_signal(barrier, inc=1, device_id=(other, chan), device_id_type=MESH)
    pl.semaphore_wait(barrier, NCHAN + 1)

    def piece(pair, dx, j):
        peer = peer_of(dx, j)
        return pltpu.make_async_remote_copy(
            src_ref=send_ref.at[pair, peer],
            dst_ref=all_ref.at[section, pair, chan],
            send_sem=out_sem.at[pair, dx],
            recv_sem=in_sem.at[pair, dx],
            device_id=(section, peer),
            device_id_type=MESH,
        )

    def block(sec, pair, dx, half=None):
        start = ((x + NX - dx) % NX) * XBLOCK
        if half is None:
            return all_ref.at[sec, pair, pl.ds(start, XBLOCK)]
        return all_ref.at[sec, pair, pl.ds(start + half * (XBLOCK // 2), XBLOCK // 2)]

    def ycopy(sec, pair, dx, half, target, slot):
        return pltpu.make_async_remote_copy(
            src_ref=block(sec, pair, dx, half),
            dst_ref=block(sec, pair, dx, half),
            send_sem=ysend_sem.at[pair, dx, slot],
            recv_sem=yin_sem.at[pair, dx, slot],
            device_id=(target, chan),
            device_id_type=MESH,
        )

    order = [(pair, dx) for pair in (1, 0) for dx in range(NX)]
    for pair in (1, 0):
        pltpu.make_async_copy(
            send_ref.at[pair, chan], all_ref.at[section, pair, chan], in_sem.at[pair, 0]
        ).start()
        for dx in range(NX):

            @pl.loop(1 if dx == 0 else 0, XBLOCK)
            def _(j):
                piece(pair, dx, j).start()

    def relay(pair, dx):
        ycopy(left, pair, dx, None, right, 0).wait_recv()
        ycopy(left, pair, dx, 0, right, 2).start()
        ycopy(right, pair, dx, None, left, 1).wait_recv()
        ycopy(right, pair, dx, 1, left, 3).start()

    for n, (pair, dx) in enumerate(order):
        mine = block(section, pair, dx)
        pltpu.make_async_copy(mine, mine, in_sem.at[pair, dx]).wait()
        ycopy(section, pair, dx, None, right, 0).start()
        ycopy(section, pair, dx, None, left, 1).start()
        if n > 0:
            relay(*order[n - 1])
    relay(*order[-1])
    far = (section + 2) % NSEC
    for pair, dx in order:
        ycopy(far, pair, dx, 0, right, 2).wait_recv()
        ycopy(far, pair, dx, 1, left, 3).wait_recv()
    for pair, dx in order:
        ycopy(section, pair, dx, None, right, 0).wait_send()
        ycopy(section, pair, dx, None, left, 1).wait_send()
        ycopy(left, pair, dx, 0, right, 2).wait_send()
        ycopy(right, pair, dx, 1, left, 3).wait_send()
        count = XBLOCK - 1 if dx == 0 else XBLOCK
        sent = send_ref.at[pair, pl.ds(0, count)]
        pltpu.make_async_copy(sent, sent, out_sem.at[pair, dx]).wait()


def products_kernel(row_ref, col_ref, all_ref, own_ref, table_ref, index_ref, vis_ref, beam_ref, weight_ref):
    def tile(index, sec, pair):
        part = all_ref[sec, pair, pl.ds(index * (TB // LOCAL), TB // LOCAL)]
        return jnp.concatenate(
            [part[:, 0].reshape(TB, NL), part[:, 1].reshape(TB, NL)], axis=0
        )

    @pl.loop(0, ITEMS)
    def _(r):
        a, b = row_ref[r], col_ref[r]
        spans = [(sec, pair) for sec in range(NSEC) for pair in range(2)]
        left = jnp.concatenate([tile(a, *span) for span in spans], axis=1)
        right = jnp.concatenate([tile(b, *span) for span in spans], axis=1)
        gram = lax.dot_general(left, right, NT, preferred_element_type=jnp.float32)
        vis_ref[0, r, 0] = (gram[:TB, :TB] + gram[TB:, TB:]) * MEAN
        vis_ref[0, r, 1] = (gram[TB:, :TB] - gram[:TB, TB:]) * MEAN

    picked = (
        lax.broadcasted_iota(jnp.int32, (NBEAM, NBEAM), 0) == index_ref[...]
    ).astype(jnp.float32).astype(jnp.bfloat16)
    chosen = lax.dot_general(
        picked, table_ref[...], TN, preferred_element_type=jnp.float32
    ).astype(jnp.bfloat16)
    for l in range(2):
        spread = (
            lax.broadcasted_iota(jnp.int32, (STATIONS, INPUTS), 1)
            == 2 * lax.broadcasted_iota(jnp.int32, (STATIONS, INPUTS), 0) + l
        ).astype(jnp.float32).astype(jnp.bfloat16)
        for q in range(2):
            weight_ref[pl.ds(q * NBEAM, NBEAM), :] = lax.dot_general(
                chosen[:, q * STATIONS : (q + 1) * STATIONS], spread, NN,
                preferred_element_type=jnp.float32,
            ).astype(jnp.bfloat16)
        for pair in range(2):
            spectra = jnp.concatenate(
                [own_ref[0, pair, :, q].reshape(INPUTS, NL) for q in range(2)], axis=1
            )
            sums = lax.dot_general(
                weight_ref[...], spectra, NN, preferred_element_type=jnp.float32
            )
            real = sums[:NBEAM, :NL] - sums[NBEAM:, NL:]
            imag = sums[:NBEAM, NL:] + sums[NBEAM:, :NL]
            power = real * real + imag * imag
            for t2 in range(2):
                beam_ref[l, :, 2 * pair + t2, :] = power[:, t2 * AVG : (t2 + 1) * AVG]


def shards(voltages, coefficients, tile_order, steer_table, beam_index):
    section = lax.axis_index("section")
    own = voltages.reshape(2, LOCAL, 4, NA, NL)
    history = lax.ppermute(own[:, :, 1:], "section", [(i, i + 1) for i in range(NSEC - 1)])
    first, twiddle, second = tables()
    vmem = pl.BlockSpec(memory_space=pltpu.VMEM)
    smem = pl.BlockSpec(memory_space=pltpu.SMEM)
    anywhere = pl.BlockSpec(memory_space=pl.ANY)
    pieces = pl.pallas_call(
        channelize_kernel,
        out_shape=jax.ShapeDtypeStruct((2, NCHAN, 2, LOCAL, NL), jnp.bfloat16),
        in_specs=[vmem] * 6,
        out_specs=vmem,
        scratch_shapes=[pltpu.VMEM((2 * NCHAN * LOCAL, NL), jnp.float32)],
        name="channelize",
    )(own, history, coefficients.reshape(TAPS, NA, NL), first, twiddle, second)
    gathered = pl.pallas_call(
        exchange_kernel,
        out_shape=jax.ShapeDtypeStruct((NSEC, 2, NCHAN, 2, LOCAL, NL), jnp.bfloat16),
        in_specs=[anywhere],
        out_specs=anywhere,
        scratch_shapes=[
            pltpu.SemaphoreType.DMA,
            pltpu.SemaphoreType.DMA((2, NX)),
            pltpu.SemaphoreType.DMA((2, NX)),
            pltpu.SemaphoreType.DMA((2, NX, 4)),
            pltpu.SemaphoreType.DMA((2, NX, 4)),
        ],
        compiler_params=pltpu.CompilerParams(collective_id=0, has_side_effects=True),
        name="exchange",
    )(pieces)
    items = lax.dynamic_slice_in_dim(tile_order[0], section * ITEMS, ITEMS)
    starts = np.array([a * (a + 1) // 2 for a in range(8)], np.int32)
    rows = jnp.sum((starts[None, :] <= items[:, None]).astype(jnp.int32), axis=1) - 1
    cols = items - rows * (rows + 1) // 2
    visibility, beam_power = pl.pallas_call(
        products_kernel,
        out_shape=(
            jax.ShapeDtypeStruct((1, ITEMS, 2, TB, TB), jnp.float32),
            jax.ShapeDtypeStruct((2, NBEAM, 4, AVG), jnp.float32),
        ),
        in_specs=[smem, smem, vmem, vmem, vmem, vmem],
        out_specs=(vmem, vmem),
        scratch_shapes=[pltpu.VMEM((2 * NBEAM, INPUTS), jnp.bfloat16)],
        name="products",
    )(
        rows,
        cols,
        gathered,
        lax.dynamic_slice_in_dim(gathered, section, 1, 0),
        steer_table.reshape(NBEAM, 2 * STATIONS),
        beam_index.reshape(1, NBEAM),
    )
    return visibility, beam_power


def solution(mesh):
    placed = (P(None, "chan", "section", None), P(), P("chan", None), P(), P(None, "chan"))
    return jax.shard_map(
        shards,
        mesh=mesh,
        in_specs=placed,
        out_specs=(P("chan", "section", None, None, None), P(None, None, "section", "chan")),
        check_vma=False,
    )
```

time: 259 us -> 112 us (0.43)
  Pallas kernels: 0 us -> 82.8 us
  waiting for transfers between devices: 90.6 us -> 11.9 us
  local copies, waits for them, and re-layouts: 85.6 us -> 11.3 us
  blocking collectives: 41.3 us -> 0 us
  between operations: 14.3 us -> 0.7 us
  matrix products: 12.9 us -> 0 us
  other arithmetic: 9 us -> 0.75 us
    pallas_call x0 -> x3, Pallas kernels: none -> 82.8 us  [the longest x1 56.6 us: shards(): pl.pallas_call(exchange_kernel, out_shape=jax.ShapeDtypeStruct((NSEC, 2,...]
    all_gather x1 -> x0, waiting for transfers between devices: 74.9 us -> none  [shards(): lax.all_gather(shard_piece, 'section', axis=2, tiled=True)]
    all_to_all x1 -> x0, blocking collectives: 41.3 us -> none  [shards(): lax.all_to_all(spectra, 'chan', split_axis=3, concat_axis=1, tiled=True)]
    unnamed x22 -> x10, local copies, waits for them, and re-layouts: 22.1 us -> 4.28 us
    convert_element_type x2 -> x0, local copies, waits for them, and re-layouts: 14.2 us -> none  [shards(): spectra = channelize(filtered.reshape(2, inputs_dev * frames_dev, NA * NB...]
    gather x3 -> x0, local copies, waits for them, and re-layouts: 13.5 us -> none  [the longest x1 5.92 us: pair_products(): jnp.take(tile_table, row_tiles * channel_groups + local_channel, axis=0)]
    dot_general x5 -> x0, matrix products: 12.9 us -> none  [the longest x1 4.15 us: channelize(): jnp.einsum('qmab,qrac->rmcb', blocks, dft_table(NA), precision=lax.Precis...]
    reshape x2 -> x1, local copies, waits for them, and re-layouts: 15 us -> 2.16 us  [shards(): own = voltages.reshape(2, LOCAL, 4, NA, NL)]
  transfers between devices with their start and end apart: 2 -> 1, of which waited for: 2 -> 1; matrix products, arithmetic and copies ran while one was open for 4% -> 4% of each run, Pallas kernels for 0% -> 0%
where the time goes in v1:
time: 112 us
  Pallas kernels  82.8 us (74%)
  waiting for transfers between devices  11.9 us (11%)
  local copies, waits for them, and re-layouts  11.3 us (10%)
  starting transfers between devices  4.07 us (4%)
    pallas_call x1, Pallas kernels, shards(): pl.pallas_call(exchange_kernel, out_shape=jax.ShapeDtypeStruct((NSEC, 2,...  56.6 us
    pallas_call x1, Pallas kernels, shards(): pl.pallas_call(channelize_kernel, out_shape=jax.ShapeDtypeStruct((2, NCHA...  15.6 us
    ppermute x1, waiting for transfers between devices, shards(): lax.ppermute(own[:, :, 1:], 'section', [(i, i + 1) for i in range(NSEC -...  11.9 us
    pallas_call x1, Pallas kernels, shards(): pl.pallas_call(products_kernel, out_shape=(jax.ShapeDtypeStruct((1, ITEMS...  10.6 us
    unnamed x10, local copies, waits for them, and re-layouts  4.28 us
    ppermute x1, starting transfers between devices, shards(): lax.ppermute(own[:, :, 1:], 'section', [(i, i + 1) for i in range(NSEC -...  4.07 us
    dynamic_slice x1, local copies, waits for them, and re-layouts, shards(): lax.dynamic_slice_in_dim(gathered, section, 1, 0)  2.34 us
    pallas_call x1, local copies, waits for them, and re-layouts, shards(): pl.pallas_call(products_kernel, out_shape=(jax.ShapeDtypeStruct((1, ITEMS...  2.34 us
  transfers between devices with their start and end apart: 1, of which 1 were waited for; matrix products, arithmetic and copies ran while one was open for 4% of the time, Pallas kernels for 0%

profile of v1, /device:TPU:1, one launch (start us, length us, event | category | flops | bytes accessed | tf_op | source)
XLA Modules:
  0.0 111.5 jit_solution(2681933575692755784)
XLA Ops:
  0.6 0.0 copy-start.3
  0.6 0.0 copy-start.2
  0.7 2.2 %reshape.19.own_ref = bf16[2,16,4,32,128]{4,3,2,1,0:T(8,128)(2,1)S(1)} reshape(bf16[2,16,4,4096]{3,2,1,0:T(4,128)(2,1)} %param.9) | data formatting | bytes 2097152 | tf_op jit(solution)/shard_map/reshape | solution.py:250
  2.8 0.0 copy-start
  2.8 0.1 slice.4
  2.9 4.1 %collective-permute-start = (bf16[2,16,3,32,128]{4,3,2,1,0:T(8,128)(2,1)S(1)}, bf16[2,16,3,32,128]{4,3,2,1,0:T(8,128)(2,1)S(1)}, u32[]{:S(2)}, u32[]{:S(2)}) collective-permute-start(bf16[2,16,3,32,128]{4,3,2,1,0:T(8,128)(2,1)S(1)} %slice.4), channel_id=1, source_target_pairs={{0,64},{64,128},{128,192},{1,65},{65,129},{129,193},{2,66},{66,130... | collective-permute-start | bytes 2359304 | tf_op jit(solution)/shard_map/ppermute | solution.py:251
  7.0 1.5 %copy.16 = f32[1,4,32,128]{3,2,1,0:T(8,128)} copy(f32[1,4,32,128]{3,1,2,0:T(4,128)} %bitcast.14) | data formatting | bytes 131072
  8.5 1.9 %copy.14 = bf16[32,8,2,512]{3,1,2,0:T(8,128)(2,1)} copy(bf16[32,8,2,512]{3,2,1,0:T(2,128)(2,1)} %bitcast.12) | data formatting | bytes 1048576
  10.4 0.0 copy-done.2
  10.4 0.1 dynamic-slice_bitcast_fusion
  10.4 0.0 copy-done.3
  10.4 0.1 convert_reduce_fusion
  10.5 0.7 fusion
  11.2 11.9 %collective-permute-done.past_ref = bf16[2,16,3,32,128]{4,3,2,1,0:T(8,128)(2,1)S(1)} collective-permute-done((bf16[2,16,3,32,128]{4,3,2,1,0:T(8,128)(2,1)S(1)}, bf16[2,16,3,32,128]{4,3,2,1,0:T(8,128)(2,1)S(1)}, u32[]{:S(2)}, u32[]{:S(2)}) %collective-permute-start) | collective-permute-done | bytes 786464 | tf_op jit(solution)/shard_map/ppermute | solution.py:251
  23.1 0.0 copy-start.1
  23.1 0.0 copy-done
  23.1 0.9 copy-done.1
  24.0 15.6 %channelize.1.send_ref = bf16[2,64,2,16,128]{4,3,2,1,0:T(8,128)(2,1)} custom-call(bf16[2,16,4,32,128]{4,3,2,1,0:T(8,128)(2,1)} %copy-done, bf16[2,16,3,32,128]{4,3,2,1,0:T(8,128)(2,1)} %copy-done.1, f32[4,32,128]{2,1,0:T(8,128)} %bitcast.13, bf16[64,192]{1,0:T(8,128)(2,1)} %constant.39.clone.first_ref, f32[2,64,128]{2,1,0:T(8,128)} %constant.40.clone.twid_ref, ...), custom_call_target="tpu_custom_call" | custom-call | tf_op jit(solution)/shard_map/channelize/pallas_call | solution.py:256
  39.7 56.6 %exchange.1.all_ref = bf16[4,2,64,2,16,128]{5,4,3,2,1,0:T(8,128)(2,1)} custom-call(bf16[2,64,2,16,128]{4,3,2,1,0:T(8,128)(2,1)} %channelize.1.send_ref), custom_call_target="tpu_custom_call" | custom-call | tf_op jit(solution)/shard_map/exchange/pallas_call | solution.py:264
  96.2 2.3 %constant_dynamic-slice_fusion.own_ref = bf16[1,2,64,2,16,128]{5,4,3,2,1,0:T(8,128)(2,1)} fusion(bf16[4,2,64,2,16,128]{5,4,3,2,1,0:T(8,128)(2,1)} %exchange.1.all_ref, s32[]{:T(128)S(6)} %select_n.13), kind=kLoop, calls=%fused_computation.8 | loop fusion | bytes 2097156 | tf_op jit(solution)/shard_map/dynamic_slice | solution.py:297
  98.6 10.6 %products.1 = (f32[1,9,2,128,128]{4,3,2,1,0:T(8,128)}, f32[2,256,4,64]{3,2,1,0:T(4,128)}) custom-call(s32[9]{0:T(128)} %get-tuple-element.7.row_ref, s32[9]{0:T(128)} %get-tuple-element.6.col_ref, bf16[4,2,64,2,16,128]{5,4,3,2,1,0:T(8,128)(2,1)} %exchange.1.all_ref, bf16[1,2,64,2,16,128]{5,4,3,2,1,0:T(8,128)(2,1)} %constant_dynamic-slice_fusion.own_ref, ...), custom_call_target="tpu_custom_call" | custom-call | tf_op jit(solution)/shard_map/products/pallas_call | solution.py:283
  109.2 2.3 %copy.12 = f32[2,256,4,64]{1,3,2,0:T(8,128)} copy(f32[2,256,4,64]{3,2,1,0:T(4,128)} %get-tuple-element.5) | data formatting | bytes 1048576 | tf_op jit(solution)/shard_map/products/pallas_call | solution.py:283
Async XLA Ops:
  0.6 9.8 %copy-start.3 = (s32[8]{0:T(128)S(1)}, s32[8]{0:T(128)}, u32[]{:S(2)}) copy-start(s32[8]{0:T(128)} %constant.46) | copy-start | bytes 100
  0.6 9.7 %copy-start.2 = (s32[1,36]{1,0:T(1,128)S(1)}, s32[1,36]{1,0:T(1,128)}, u32[]{:S(2)}) copy-start(s32[1,36]{1,0:T(1,128)} %param.11) | copy-start | bytes 436
  2.8 20.3 %copy-start = (bf16[2,16,4,32,128]{4,3,2,1,0:T(8,128)(2,1)}, bf16[2,16,4,32,128]{4,3,2,1,0:T(8,128)(2,1)S(1)}, u32[]{:S(2)}) copy-start(bf16[2,16,4,32,128]{4,3,2,1,0:T(8,128)(2,1)S(1)} %reshape.19.own_ref) | copy-start | bytes 3145732
  2.9 20.2 %collective-permute-start = (bf16[2,16,3,32,128]{4,3,2,1,0:T(8,128)(2,1)S(1)}, bf16[2,16,3,32,128]{4,3,2,1,0:T(8,128)(2,1)S(1)}, u32[]{:S(2)}, u32[]{:S(2)}) collective-permute-start(bf16[2,16,3,32,128]{4,3,2,1,0:T(8,128)(2,1)S(1)} %slice.4), channel_id=1, source_target_pairs={{0,64},{64,128},{128,192},{1,65},{65,129},{129,193},{2,66},{66,130... | collective-permute-start | bytes 2359304 | tf_op jit(solution)/shard_map/ppermute | solution.py:251
  23.1 0.9 copy-start.1

commit v2 on v1

v2 whole, which is shorter than its diff:
```python
import jax
import jax.numpy as jnp
import ml_dtypes
import numpy as np
from jax import lax
from jax.experimental import pallas as pl
from jax.experimental.pallas import tpu as pltpu
from jax.sharding import PartitionSpec as P

NSEC = 4
NX, NZ, NCORE = 4, 8, 2
NCHAN = NX * NZ * NCORE
XBLOCK = NZ * NCORE
LOCAL = 16
NCH = 4096
TAPS = 4
NA = 32
NL = 128
AVG = 64
TB = 128
ITEMS = 9
UNROLL = 4
NBEAM = 256
STATIONS = 512
INPUTS = 1024
MEAN = 1.0 / 1024.0
NT = (((1,), (1,)), ((), ()))
NN = (((1,), (0,)), ((), ()))
TN = (((0,), (0,)), ((), ()))
MESH = pl.DeviceIdType.MESH


def split_np(table):
    high = table.astype(ml_dtypes.bfloat16)
    low = (table - high.astype(np.float64)).astype(ml_dtypes.bfloat16)
    return high, low


def tables():
    c = np.arange(NA)
    angle = 2.0 * np.pi / NA * ((c[:, None] * c[None, :]) % NA)
    cosine, sine = np.cos(angle), np.sin(angle)
    first = np.block([[cosine, sine], [-sine, cosine]])
    high, low = split_np(first)
    first = np.concatenate([high, low, high], axis=1)
    channel = np.arange(AVG)
    lane = np.arange(NL)
    angle = 2.0 * np.pi / NCH * ((channel[:, None] * lane[None, :]) % NCH)
    twiddle = np.stack([np.cos(angle), np.sin(angle)]).astype(np.float32)
    group = np.arange(NCHAN)
    angle = 2.0 * np.pi / NCHAN * ((group[:, None] * lane[None, :]) % NCHAN)
    cosine, sine = np.cos(angle), np.sin(angle)
    second = np.stack(
        [np.concatenate([cosine, sine], axis=1), np.concatenate([-sine, cosine], axis=1)], axis=1
    ).reshape(2 * NCHAN, 2 * NL)
    high, low = split_np(second)
    second = np.concatenate([high, low, high], axis=1)
    return jnp.asarray(first), jnp.asarray(twiddle), jnp.asarray(second)


def split(value):
    high = value.astype(jnp.bfloat16)
    return high, (value - high.astype(jnp.float32)).astype(jnp.bfloat16)


def stage_one(frame, t2, sources, coef_ref, first_ref, twid_ref, turned_ref):
    @pl.loop(0, LOCAL, step=UNROLL)
    def _(start):
        columns = []
        for u in range(UNROLL):
            parts = []
            for q in range(2):
                total = None
                for p in range(TAPS):
                    term = coef_ref[pl.ds(p * NA, NA), :] * sources(q, start + u, frame - p).astype(jnp.float32)
                    total = term if total is None else total + term
                parts.append(total)
            columns.append(jnp.concatenate(parts, axis=0))
        high, low = split(jnp.concatenate(columns, axis=1))
        section_one = lax.dot_general(
            first_ref[...],
            jnp.concatenate([high, high, low], axis=0),
            NN,
            preferred_element_type=jnp.float32,
        )
        cosine, sine = twid_ref[0], twid_ref[1]
        for u in range(UNROLL):
            real = section_one[:NA, u * NL : (u + 1) * NL]
            imag = section_one[NA:, u * NL : (u + 1) * NL]
            real = jnp.concatenate([real, real], axis=0)
            imag = jnp.concatenate([imag, imag], axis=0)
            high, low = split(
                jnp.concatenate([real * cosine + imag * sine, imag * cosine - real * sine], axis=1)
            )
            turned_ref[start + u, t2 * AVG : (t2 + 1) * AVG, :] = jnp.concatenate([high, low], axis=1)


def stage_two(pair, second_ref, turned_ref, rows_ref, send_ref):
    @pl.loop(0, LOCAL, step=UNROLL)
    def _(start):
        turned = turned_ref[pl.ds(start, UNROLL)].reshape(UNROLL * 2 * AVG, 4 * NL)
        high, low = turned[:, : 2 * NL], turned[:, 2 * NL :]
        section_two = lax.dot_general(
            second_ref[...],
            jnp.concatenate([high, high, low], axis=1),
            NT,
            preferred_element_type=jnp.float32,
        )
        for u in range(UNROLL):
            rows_ref[pl.ds(start + u, 2 * NCHAN, stride=LOCAL), :] = section_two[
                :, u * NL : (u + 1) * NL
            ]

    send_ref[pair] = rows_ref[...].astype(jnp.bfloat16).reshape(NCHAN, 2, LOCAL, NL)


def tile(buffer, index):
    part = buffer[pl.ds(index * (TB // LOCAL), TB // LOCAL)]
    return jnp.concatenate([part[:, 0].reshape(TB, NL), part[:, 1].reshape(TB, NL)], axis=0)


def correlator_kernel(
    own_ref, coefs_ref, first_ref, twid_ref, second_ref, order_ref, table_ref, index_ref,
    vis_ref, beam_ref,
    past_ref, coef_ref, turned_ref, rows_ref, send_ref, mine1, left1, right1, far1,
    mine0, left0, right0, far0, acc_ref, weight_ref,
    past_send, past_recv, out_sem, in_sem, ysend_sem, yin_sem,
):
    section = lax.axis_index("section")
    chan = lax.axis_index("chan")
    x, z, core = chan // XBLOCK, (chan % XBLOCK) // NCORE, chan % NCORE
    right, left = (section + 1) % NSEC, (section + NSEC - 1) % NSEC
    mine, lefts, rights, fars = (mine0, mine1), (left0, left1), (right0, right1), (far0, far1)

    barrier = pltpu.get_barrier_semaphore()

    @pl.loop(1, NCHAN)
    def _(k):
        pl.semaphore_signal(
            barrier, inc=1, device_id=(section, (chan + k) % NCHAN), device_id_type=MESH
        )

    for other in (left, right):
        pl.semaphore_signal(barrier, inc=1, device_id=(other, chan), device_id_type=MESH)

    for a in range(NA):
        coef_ref[pl.ds(a, TAPS, stride=NA), :] = coefs_ref[:, a * NL : (a + 1) * NL]

    def sources(q, i, t):
        return own_ref[q, i, t] if t >= 0 else past_ref[t + TAPS - 1, q, i]

    stage_one(3, 1, sources, coef_ref, first_ref, twid_ref, turned_ref)
    pl.semaphore_wait(barrier, NCHAN + 1)

    def halo(t):
        return pltpu.make_async_remote_copy(
            src_ref=own_ref.at[:, :, t + 4],
            dst_ref=past_ref.at[t + TAPS - 1],
            send_sem=past_send.at[t + TAPS - 1],
            recv_sem=past_recv.at[t + TAPS - 1],
            device_id=(right, chan),
            device_id_type=MESH,
        )

    def halo_wait(t):
        halo(t).wait_recv()

        @pl.when(section == 0)
        def _():
            past_ref[t + TAPS - 1] = jnp.zeros(past_ref.shape[1:], jnp.bfloat16)

    for t in (-1, -2, -3):
        halo(t).start()

    def piece(pair, dx, j):
        dz, dc = j // NCORE, j % NCORE
        peer = ((x + dx) % NX) * XBLOCK + ((z + dz) % NZ) * NCORE + (core + dc) % NCORE
        return pltpu.make_async_remote_copy(
            src_ref=send_ref.at[pair, peer],
            dst_ref=mine[pair].at[chan],
            send_sem=out_sem.at[pair, dx],
            recv_sem=in_sem.at[pair, dx],
            device_id=(section, peer),
            device_id_type=MESH,
        )

    def scatter(pair):
        pltpu.make_async_copy(
            send_ref.at[pair, chan], mine[pair].at[chan], in_sem.at[pair, 0]
        ).start()
        for dx in range(NX):

            @pl.loop(1 if dx == 0 else 0, XBLOCK)
            def _(j):
                piece(pair, dx, j).start()

    def ycopy(source, target, dx, half, peer, pair, slot):
        start = ((x + NX - dx) % NX) * XBLOCK
        count = XBLOCK
        if half is not None:
            count = XBLOCK // 2
            start = start + half * count
        return pltpu.make_async_remote_copy(
            src_ref=source[pair].at[pl.ds(start, count)],
            dst_ref=target[pair].at[pl.ds(start, count)],
            send_sem=ysend_sem.at[pair, dx, slot],
            recv_sem=yin_sem.at[pair, dx, slot],
            device_id=(peer, chan),
            device_id_type=MESH,
        )

    def to_right(pair, dx):
        return ycopy(mine, lefts, dx, None, right, pair, 0)

    def to_left(pair, dx):
        return ycopy(mine, rights, dx, None, left, pair, 1)

    def on_right(pair, dx):
        return ycopy(lefts, fars, dx, 0, right, pair, 2)

    def on_left(pair, dx):
        return ycopy(rights, fars, dx, 1, left, pair, 3)

    def forward(pair, dx):
        part = mine[pair].at[pl.ds(((x + NX - dx) % NX) * XBLOCK, XBLOCK)]
        pltpu.make_async_copy(part, part, in_sem.at[pair, dx]).wait()
        to_right(pair, dx).start()
        to_left(pair, dx).start()

    def relay(pair, dx):
        to_right(pair, dx).wait_recv()
        on_right(pair, dx).start()
        to_left(pair, dx).wait_recv()
        on_left(pair, dx).start()

    def far_wait(pair):
        for dx in range(NX):
            on_right(pair, dx).wait_recv()
            on_left(pair, dx).wait_recv()

    def products(buffers, first, last):
        @pl.loop(0, ITEMS)
        def _(r):
            n = order_ref[0, section * ITEMS + r]
            a = 0
            for k in range(1, INPUTS // TB):
                a = a + (n >= k * (k + 1) // 2).astype(jnp.int32)
            b = n - a * (a + 1) // 2
            gram = lax.dot_general(
                jnp.concatenate([tile(buffer, a) for buffer in buffers], axis=1),
                jnp.concatenate([tile(buffer, b) for buffer in buffers], axis=1),
                NT,
                preferred_element_type=jnp.float32,
            )
            if not first:
                gram = gram + acc_ref[r]
            if last:
                vis_ref[0, r, 0] = (gram[:TB, :TB] + gram[TB:, TB:]) * MEAN
                vis_ref[0, r, 1] = (gram[TB:, :TB] - gram[:TB, TB:]) * MEAN
            else:
                acc_ref[r] = gram

    def weights():
        picked = (
            lax.broadcasted_iota(jnp.int32, (NBEAM, NBEAM), 0) == index_ref[...]
        ).astype(jnp.float32).astype(jnp.bfloat16)
        chosen = lax.dot_general(
            picked, table_ref[...], TN, preferred_element_type=jnp.float32
        ).astype(jnp.bfloat16)
        for l in range(2):
            spread = (
                lax.broadcasted_iota(jnp.int32, (STATIONS, INPUTS), 1)
                == 2 * lax.broadcasted_iota(jnp.int32, (STATIONS, INPUTS), 0) + l
            ).astype(jnp.float32).astype(jnp.bfloat16)
            for q in range(2):
                weight_ref[l, pl.ds(q * NBEAM, NBEAM), :] = lax.dot_general(
                    chosen[:, q * STATIONS : (q + 1) * STATIONS], spread, NN,
                    preferred_element_type=jnp.float32,
                ).astype(jnp.bfloat16)

    def beams(pair, l):
        spectra = jnp.concatenate(
            [mine[pair][:, q].reshape(INPUTS, NL) for q in range(2)], axis=1
        )
        sums = lax.dot_general(weight_ref[l], spectra, NN, preferred_element_type=jnp.float32)
        real = sums[:NBEAM, :NL] - sums[NBEAM:, NL:]
        imag = sums[:NBEAM, NL:] + sums[NBEAM:, :NL]
        power = (real * real + imag * imag).T
        for t2 in range(2):
            beam_ref[l, 2 * pair + t2] = power[t2 * AVG : (t2 + 1) * AVG]

    halo_wait(-1)
    stage_one(2, 0, sources, coef_ref, first_ref, twid_ref, turned_ref)
    stage_two(1, second_ref, turned_ref, rows_ref, send_ref)
    scatter(1)
    halo_wait(-2)
    stage_one(1, 1, sources, coef_ref, first_ref, twid_ref, turned_ref)
    forward(1, 0)
    halo_wait(-3)
    stage_one(0, 0, sources, coef_ref, first_ref, twid_ref, turned_ref)
    forward(1, 1)
    relay(1, 0)
    stage_two(0, second_ref, turned_ref, rows_ref, send_ref)
    scatter(0)
    forward(1, 2)
    relay(1, 1)
    forward(1, 3)
    relay(1, 2)
    weights()
    forward(0, 0)
    relay(1, 3)
    beams(1, 0)
    forward(0, 1)
    relay(0, 0)
    beams(1, 1)
    forward(0, 2)
    relay(0, 1)
    products((mine1, left1, right1), True, False)
    forward(0, 3)
    relay(0, 2)
    far_wait(1)
    products((far1, mine0), False, False)
    relay(0, 3)
    products((left0, right0), False, False)
    beams(0, 0)
    beams(0, 1)
    far_wait(0)
    products((far0,), False, True)

    for t in (-1, -2, -3):
        halo(t).wait_send()
    for pair in (1, 0):
        for dx in range(NX):
            for copy in (to_right, to_left, on_right, on_left):
                copy(pair, dx).wait_send()
            sent = send_ref.at[pair, pl.ds(0, XBLOCK - 1 if dx == 0 else XBLOCK)]
            pltpu.make_async_copy(sent, sent, out_sem.at[pair, dx]).wait()


def shards(voltages, coefficients, tile_order, steer_table, beam_index):
    vmem = pl.BlockSpec(memory_space=pltpu.VMEM)
    smem = pl.BlockSpec(memory_space=pltpu.SMEM)
    frames = pltpu.VMEM((NCHAN, 2, LOCAL, NL), jnp.bfloat16)
    visibility, beam_power = pl.pallas_call(
        correlator_kernel,
        out_shape=(
            jax.ShapeDtypeStruct((1, ITEMS, 2, TB, TB), jnp.float32),
            jax.ShapeDtypeStruct((2, 4, AVG, NBEAM), jnp.float32),
        ),
        in_specs=[vmem, vmem, vmem, vmem, vmem, smem, vmem, vmem],
        out_specs=(vmem, vmem),
        scratch_shapes=[
            pltpu.VMEM((TAPS - 1, 2, LOCAL, NA, NL), jnp.bfloat16),
            pltpu.VMEM((TAPS * NA, NL), jnp.float32),
            pltpu.VMEM((LOCAL, 2 * AVG, 4 * NL), jnp.bfloat16),
            pltpu.VMEM((2 * NCHAN * LOCAL, NL), jnp.float32),
            pltpu.VMEM((2, NCHAN, 2, LOCAL, NL), jnp.bfloat16),
        ]
        + [frames] * 8
        + [
            pltpu.VMEM((ITEMS, 2 * TB, 2 * TB), jnp.float32),
            pltpu.VMEM((2, 2 * NBEAM, INPUTS), jnp.bfloat16),
            pltpu.SemaphoreType.DMA((TAPS - 1,)),
            pltpu.SemaphoreType.DMA((TAPS - 1,)),
            pltpu.SemaphoreType.DMA((2, NX)),
            pltpu.SemaphoreType.DMA((2, NX)),
            pltpu.SemaphoreType.DMA((2, NX, 4)),
            pltpu.SemaphoreType.DMA((2, NX, 4)),
        ],
        compiler_params=pltpu.CompilerParams(
            collective_id=0, has_side_effects=True, vmem_limit_bytes=48 * 1024 * 1024
        ),
        name="correlator",
    )(
        voltages.reshape(2, LOCAL, 4, NA, NL),
        coefficients,
        *tables(),
        tile_order,
        steer_table.reshape(NBEAM, 2 * STATIONS),
        beam_index.reshape(1, NBEAM),
    )
    return visibility, jnp.transpose(beam_power, (0, 3, 1, 2))


def solution(mesh):
    placed = (P(None, "chan", "section", None), P(), P("chan", None), P(), P(None, "chan"))
    return jax.shard_map(
        shards,
        mesh=mesh,
        in_specs=placed,
        out_specs=(P("chan", "section", None, None, None), P(None, None, "section", "chan")),
        check_vma=False,
    )
```

time: 112 us -> 75.7 us (0.68)
  Pallas kernels: 82.8 us -> 70 us
  waiting for transfers between devices: 11.9 us -> 0 us
  local copies, waits for them, and re-layouts: 11.3 us -> 4.24 us
  starting transfers between devices: 4.07 us -> 0 us
    pallas_call x3 -> x1, Pallas kernels: 82.8 us -> 70 us  [shards(): pl.pallas_call(correlator_kernel, out_shape=(jax.ShapeDtypeStruct((1, ITE...]
    ppermute x1 -> x0, waiting for transfers between devices: 11.9 us -> none  [shards(): lax.ppermute(own[:, :, 1:], 'section', [(i, i + 1) for i in range(NSEC -...]
    ppermute x1 -> x0, starting transfers between devices: 4.07 us -> none  [shards(): lax.ppermute(own[:, :, 1:], 'section', [(i, i + 1) for i in range(NSEC -...]
    dynamic_slice x1 -> x0, local copies, waits for them, and re-layouts: 2.34 us -> none  [shards(): lax.dynamic_slice_in_dim(gathered, section, 1, 0)]
    pallas_call x1 -> x0, local copies, waits for them, and re-layouts: 2.34 us -> none  [shards(): pl.pallas_call(products_kernel, out_shape=(jax.ShapeDtypeStruct((1, ITEMS...]
    unnamed x10 -> x17, local copies, waits for them, and re-layouts: 4.28 us -> 3.14 us
  transfers between devices with their start and end apart: 1 -> 0, of which waited for: 1 -> 0; matrix products, arithmetic and copies ran while one was open for 4% -> 0% of each run, Pallas kernels for 0% -> 0%
where the time goes in v2:
time: 75.7 us; the launch traced here: 75 us
  Pallas kernels  70 us (92%)
  local copies, waits for them, and re-layouts  4.24 us (6%)
  between operations  0.76 us (1%)
    pallas_call x1, Pallas kernels, shards(): pl.pallas_call(correlator_kernel, out_shape=(jax.ShapeDtypeStruct((1, ITE...  70 us
    unnamed x17, local copies, waits for them, and re-layouts  3.14 us

profile of v2, /device:TPU:1, one launch (start us, length us, event | category | flops | bytes accessed | tf_op | source)
XLA Modules:
  0.0 75.0 jit_solution(5495000918454126755)
XLA Ops:
  0.6 0.0 copy-start.6
  0.6 1.2 %copy.10 = bf16[32,8,2,512]{3,1,2,0:T(8,128)(2,1)S(1)} copy(bf16[32,8,2,512]{3,2,1,0:T(2,128)(2,1)} %bitcast.7) | data formatting | bytes 1048576
  1.8 0.0 copy-start
  1.9 0.0 copy-start.1
  1.9 0.0 copy-start.2
  1.9 0.0 copy-start.3
  1.9 0.0 copy-start.4
  1.9 0.0 copy-start.5
  1.9 0.1 copy-done.6
  2.0 1.1 %reshape.13.own_ref = bf16[2,16,4,32,128]{4,3,2,1,0:T(8,128)(2,1)S(1)} reshape(bf16[2,16,4,4096]{3,2,1,0:T(4,128)(2,1)S(1)} %copy-done.6) | data formatting | bytes 2097152 | tf_op jit(solution)/shard_map/reshape | solution.py:375
  3.1 0.0 copy-done
  3.1 0.0 copy-done.1
  3.1 0.0 copy-done.2
  3.2 0.0 copy-done.3
  3.2 0.0 copy-done.4
  3.2 0.0 copy-done.5
  3.2 70.0 %correlator.1 = (f32[1,9,2,128,128]{4,3,2,1,0:T(8,128)S(1)}, f32[2,4,64,256]{3,2,1,0:T(8,128)S(1)}) custom-call(bf16[2,16,4,32,128]{4,3,2,1,0:T(8,128)(2,1)S(1)} %reshape.13.own_ref, f32[4,4096]{1,0:T(4,128)S(1)} %copy-done.1, bf16[64,192]{1,0:T(8,128)(2,1)S(1)} %copy-done.3, f32[2,64,128]{2,1,0:T(8,128)S(1)} %copy-done.2, bf16[128,768]{1,0:T(8,128)(2,1)S(1)} %copy-done, ...), custom_call_target="tpu_custom_call" | custom-call | tf_op jit(solution)/shard_map/correlator/pallas_call | solution.py:344
  73.2 1.0 %copy.13 = f32[1,9,2,128,128]{4,3,2,1,0:T(8,128)} copy(f32[1,9,2,128,128]{4,3,2,1,0:T(8,128)S(1)} %get-tuple-element.8) | data formatting | bytes 2359296
  74.3 0.8 %copy.14 = f32[2,256,4,64]{1,3,2,0:T(8,128)} copy(f32[2,256,4,64]{1,3,2,0:T(8,128)S(1)} %bitcast.5) | data formatting | bytes 1048576
Async XLA Ops:
  0.6 1.4 %copy-start.6 = (bf16[2,16,4,4096]{3,2,1,0:T(4,128)(2,1)S(1)}, bf16[2,16,4,4096]{3,2,1,0:T(4,128)(2,1)}, u32[]{:S(2)}) copy-start(bf16[2,16,4,4096]{3,2,1,0:T(4,128)(2,1)} %param.8) | copy-start | bytes 3145732
  1.8 1.3 %copy-start = (bf16[128,768]{1,0:T(8,128)(2,1)S(1)}, bf16[128,768]{1,0:T(8,128)(2,1)}, u32[]{:S(2)}) copy-start(bf16[128,768]{1,0:T(8,128)(2,1)} %constant.8.clone.second_ref) | copy-start | bytes 589828
  1.9 1.3 %copy-start.1 = (f32[4,4096]{1,0:T(4,128)S(1)}, f32[4,4096]{1,0:T(4,128)}, u32[]{:S(2)}) copy-start(f32[4,4096]{1,0:T(4,128)} %coefs_ref.1) | copy-start | bytes 196612
  1.9 1.3 %copy-start.2 = (f32[2,64,128]{2,1,0:T(8,128)S(1)}, f32[2,64,128]{2,1,0:T(8,128)}, u32[]{:S(2)}) copy-start(f32[2,64,128]{2,1,0:T(8,128)} %constant.7.clone.twid_ref) | copy-start | bytes 196612
  1.9 1.3 %copy-start.3 = (bf16[64,192]{1,0:T(8,128)(2,1)S(1)}, bf16[64,192]{1,0:T(8,128)(2,1)}, u32[]{:S(2)}) copy-start(bf16[64,192]{1,0:T(8,128)(2,1)} %constant.6.clone.first_ref) | copy-start | bytes 73732
  1.9 1.3 %copy-start.4 = (s32[256,1]{0,1:T(1,128)S(1)}, s32[256,1]{0,1:T(1,128)}, u32[]{:S(2)}) copy-start(s32[256,1]{0,1:T(1,128)} %param.12) | copy-start | bytes 3076
  1.9 1.3 %copy-start.5 = (s32[1,36]{1,0:T(1,128)S(1)}, s32[1,36]{1,0:T(1,128)}, u32[]{:S(2)}) copy-start(s32[1,36]{1,0:T(1,128)} %order_ref.1) | copy-start | bytes 436

commit v3 on v2

v3 whole, which is shorter than its diff:
```python
import jax
import jax.numpy as jnp
import ml_dtypes
import numpy as np
from jax import lax
from jax.experimental import pallas as pl
from jax.experimental.pallas import tpu as pltpu
from jax.sharding import PartitionSpec as P

NSEC = 4
FRAMES = 4
NX, NZ, NCORE = 4, 8, 2
NCHAN = NX * NZ * NCORE
XBLOCK = NZ * NCORE
LOCAL = 16
NCH = 4096
TAPS = 4
NA = 32
NL = 128
AVG = 64
TB = 128
ITEMS = 9
UNROLL = 4
NBEAM = 256
STATIONS = 512
INPUTS = 1024
MEAN = 1.0 / 1024.0
NT = (((1,), (1,)), ((), ()))
NN = (((1,), (0,)), ((), ()))
TN = (((0,), (0,)), ((), ()))
MESH = pl.DeviceIdType.MESH
BY_RIGHT = ((0, 1), (0, 3))


def split_np(table):
    high = table.astype(ml_dtypes.bfloat16)
    low = (table - high.astype(np.float64)).astype(ml_dtypes.bfloat16)
    return high, low


def tables():
    c = np.arange(NA)
    angle = 2.0 * np.pi / NA * ((c[:, None] * c[None, :]) % NA)
    cosine, sine = np.cos(angle), np.sin(angle)
    first = np.block([[cosine, sine], [-sine, cosine]])
    high, low = split_np(first)
    first = np.concatenate([high, low, high], axis=1)
    channel = np.arange(AVG)
    lane = np.arange(NL)
    angle = 2.0 * np.pi / NCH * ((channel[:, None] * lane[None, :]) % NCH)
    twiddle = np.stack([np.cos(angle), np.sin(angle)]).astype(np.float32)
    group = np.arange(NCHAN)
    angle = 2.0 * np.pi / NCHAN * ((group[:, None] * lane[None, :]) % NCHAN)
    cosine, sine = np.cos(angle), np.sin(angle)
    second = np.concatenate([cosine, sine], axis=1)
    high, low = split_np(second)
    second = np.concatenate([high, low, high], axis=1)
    return jnp.asarray(first), jnp.asarray(twiddle), jnp.asarray(second)


def split(value):
    high = value.astype(jnp.bfloat16)
    return high, (value - high.astype(jnp.float32)).astype(jnp.bfloat16)


def transform(frame, lower, upper, sources, coef_ref, first_ref, twid_ref, second_ref, rows_ref):
    @pl.loop(lower, upper, step=UNROLL)
    def _(start):
        columns = []
        for u in range(UNROLL):
            parts = []
            for q in range(2):
                total = None
                for p in range(TAPS):
                    term = coef_ref[pl.ds(p * NA, NA), :] * sources(q, start + u, frame - p).astype(jnp.float32)
                    total = term if total is None else total + term
                parts.append(total)
            columns.append(jnp.concatenate(parts, axis=0))
        high, low = split(jnp.concatenate(columns, axis=1))
        section_one = lax.dot_general(
            first_ref[...],
            jnp.concatenate([high, high, low], axis=0),
            NN,
            preferred_element_type=jnp.float32,
        )
        cosine, sine = twid_ref[0], twid_ref[1]
        turned = []
        for u in range(UNROLL):
            real = section_one[:NA, u * NL : (u + 1) * NL]
            imag = section_one[NA:, u * NL : (u + 1) * NL]
            real = jnp.concatenate([real, real], axis=0)
            imag = jnp.concatenate([imag, imag], axis=0)
            real, imag = real * cosine + imag * sine, imag * cosine - real * sine
            rows = jnp.concatenate(
                [jnp.concatenate([real, imag], axis=1), jnp.concatenate([imag, -real], axis=1)], axis=0
            )
            high, low = split(rows)
            turned.append(jnp.concatenate([high, high, low], axis=1))
        section_two = lax.dot_general(
            second_ref[...],
            jnp.concatenate(turned, axis=0),
            NT,
            preferred_element_type=jnp.float32,
        )
        for u in range(UNROLL):
            rows_ref[pl.ds(start + u, NCHAN, stride=LOCAL), :] = section_two[
                :, u * NL : (u + 1) * NL
            ]


def tile(buffer, index):
    return buffer[pl.ds(index * (TB // LOCAL), TB // LOCAL)].reshape(TB, NL)


def turned_tile(buffer, index):
    part = tile(buffer, index)
    return jnp.concatenate([part[:, AVG:], -part[:, :AVG]], axis=1)


def multiply(item, buffers, acc_ref, vis_ref, order_ref, offset, first, last):
    n = order_ref[0, offset + item]
    a = 0
    for k in range(1, INPUTS // TB):
        a = a + (n >= k * (k + 1) // 2).astype(jnp.int32)
    b = n - a * (a + 1) // 2
    straight = jnp.concatenate([tile(buffer, a) for buffer in buffers], axis=1)
    turned = jnp.concatenate([turned_tile(buffer, a) for buffer in buffers], axis=1)
    gram = lax.dot_general(
        jnp.concatenate([straight, turned], axis=0),
        jnp.concatenate([tile(buffer, b) for buffer in buffers], axis=1),
        NT,
        preferred_element_type=jnp.float32,
    )
    if not first:
        gram = gram + acc_ref[item]
    if last:
        vis_ref[0, item] = (gram * MEAN).reshape(2, TB, TB)
    else:
        acc_ref[item] = gram


def make_weights(l, table_ref, index_ref, weight_ref):
    picked = (
        lax.broadcasted_iota(jnp.int32, (NBEAM, NBEAM), 0) == index_ref[...]
    ).astype(jnp.float32).astype(jnp.bfloat16)
    chosen = lax.dot_general(
        picked, table_ref[...], TN, preferred_element_type=jnp.float32
    ).astype(jnp.bfloat16)
    spread = (
        lax.broadcasted_iota(jnp.int32, (STATIONS, INPUTS), 1)
        == 2 * lax.broadcasted_iota(jnp.int32, (STATIONS, INPUTS), 0) + l
    ).astype(jnp.float32).astype(jnp.bfloat16)
    for q in range(2):
        weight_ref[l, pl.ds(q * NBEAM, NBEAM), :] = lax.dot_general(
            chosen[:, q * STATIONS : (q + 1) * STATIONS], spread, NN,
            preferred_element_type=jnp.float32,
        ).astype(jnp.bfloat16)


def form_beams(frames, l, mine, weight_ref, beam_ref):
    spectra = jnp.concatenate([mine[frame][...].reshape(INPUTS, NL) for frame in frames], axis=1)
    sums = lax.dot_general(weight_ref[l], spectra, NN, preferred_element_type=jnp.float32)
    for n, frame in enumerate(frames):
        straight = sums[:NBEAM, n * NL : (n + 1) * NL]
        crossed = sums[NBEAM:, n * NL : (n + 1) * NL]
        crossed = jnp.concatenate([-crossed[:, AVG:], crossed[:, :AVG]], axis=1)
        voltage = straight + crossed
        power = (voltage * voltage).T
        beam_ref[l, frame] = power[:AVG] + power[AVG:]


def correlator_kernel(
    own_ref, coefs_ref, first_ref, twid_ref, second_ref, order_ref, table_ref, index_ref,
    vis_ref, beam_ref,
    past_ref, coef_ref, rows_ref, send_ref,
    mine0, mine1, mine2, mine3, left0, left1, left2, left3,
    right0, right1, right2, right3, far0, far1, far2, far3,
    acc_ref, weight_ref,
    past_send, past_recv, out_sem, in_sem, ysend_sem, yin_sem,
):
    section = lax.axis_index("section")
    chan = lax.axis_index("chan")
    x, z, core = chan // XBLOCK, (chan % XBLOCK) // NCORE, chan % NCORE
    right, left = (section + 1) % NSEC, (section + NSEC - 1) % NSEC
    mine, lefts = (mine0, mine1, mine2, mine3), (left0, left1, left2, left3)
    rights, fars = (right0, right1, right2, right3), (far0, far1, far2, far3)

    barrier = pltpu.get_barrier_semaphore()

    @pl.loop(1, NCHAN)
    def _(k):
        pl.semaphore_signal(
            barrier, inc=1, device_id=(section, (chan + k) % NCHAN), device_id_type=MESH
        )

    for other in (left, right):
        pl.semaphore_signal(barrier, inc=1, device_id=(other, chan), device_id_type=MESH)

    for a in range(NA):
        coef_ref[pl.ds(a, TAPS, stride=NA), :] = coefs_ref[:, a * NL : (a + 1) * NL]

    def sources(q, i, t):
        return own_ref[q, i, t] if t >= 0 else past_ref[t + TAPS - 1, q, i]

    def fft(frame, lower, upper):
        transform(
            frame, lower, upper, sources, coef_ref, first_ref, twid_ref, second_ref, rows_ref
        )

    def halo(t):
        return pltpu.make_async_remote_copy(
            src_ref=own_ref.at[:, :, t + FRAMES],
            dst_ref=past_ref.at[t + TAPS - 1],
            send_sem=past_send.at[t + TAPS - 1],
            recv_sem=past_recv.at[t + TAPS - 1],
            device_id=(right, chan),
            device_id_type=MESH,
        )

    def halo_wait(t):
        halo(t).wait_recv()

        @pl.when(section == 0)
        def _():
            past_ref[t + TAPS - 1] = jnp.zeros(past_ref.shape[1:], jnp.bfloat16)

    def piece(frame, dx, j):
        dz, dc = j // NCORE, j % NCORE
        peer = ((x + dx) % NX) * XBLOCK + ((z + dz) % NZ) * NCORE + (core + dc) % NCORE
        return pltpu.make_async_remote_copy(
            src_ref=send_ref.at[frame, peer],
            dst_ref=mine[frame].at[chan],
            send_sem=out_sem.at[frame, dx],
            recv_sem=in_sem.at[frame, dx],
            device_id=(section, peer),
            device_id_type=MESH,
        )

    def scatter(frame):
        send_ref[frame] = rows_ref[...].astype(jnp.bfloat16).reshape(NCHAN, LOCAL, NL)
        pltpu.make_async_copy(
            send_ref.at[frame, chan], mine[frame].at[chan], in_sem.at[frame, 0]
        ).start()
        for dx in range(NX):

            @pl.loop(1 if dx == 0 else 0, XBLOCK)
            def _(j):
                piece(frame, dx, j).start()

    def ycopy(source, target, dx, peer, frame, slot):
        part = pl.ds(((x + NX - dx) % NX) * XBLOCK, XBLOCK)
        return pltpu.make_async_remote_copy(
            src_ref=source[frame].at[part],
            dst_ref=target[frame].at[part],
            send_sem=ysend_sem.at[frame, dx, slot],
            recv_sem=yin_sem.at[frame, dx, slot],
            device_id=(peer, chan),
            device_id_type=MESH,
        )

    def to_right(frame, dx):
        return ycopy(mine, lefts, dx, right, frame, 0)

    def to_left(frame, dx):
        return ycopy(mine, rights, dx, left, frame, 1)

    def onward(frame, dx):
        if (frame, dx) in BY_RIGHT:
            return ycopy(lefts, fars, dx, right, frame, 2)
        return ycopy(rights, fars, dx, left, frame, 2)

    def forward(frame, dx):
        part = mine[frame].at[pl.ds(((x + NX - dx) % NX) * XBLOCK, XBLOCK)]
        pltpu.make_async_copy(part, part, in_sem.at[frame, dx]).wait()
        to_left(frame, dx).start()
        to_right(frame, dx).start()

    def relay(frame, dx):
        (to_right if (frame, dx) in BY_RIGHT else to_left)(frame, dx).wait_recv()
        onward(frame, dx).start()

    def near_wait(frame):
        for dx in range(NX):
            (to_left if (frame, dx) in BY_RIGHT else to_right)(frame, dx).wait_recv()

    def far_wait(frame):
        for dx in range(NX):
            onward(frame, dx).wait_recv()

    def products(buffers, first=False, last=False):
        @pl.loop(0, ITEMS)
        def _(item):
            multiply(
                item, buffers, acc_ref, vis_ref, order_ref, section * ITEMS, first, last
            )

    def weights(l):
        make_weights(l, table_ref, index_ref, weight_ref)

    def beams(frames, l):
        form_beams(frames, l, mine, weight_ref, beam_ref)

    half = LOCAL // 2
    fft(3, 0, LOCAL)
    pl.semaphore_wait(barrier, NCHAN + 1)
    for t in (-1, -2, -3):
        halo(t).start()
    scatter(3)
    forward(3, 0)
    weights(0)
    forward(3, 1)
    weights(1)
    forward(3, 2)
    relay(3, 0)
    forward(3, 3)
    relay(3, 1)
    halo_wait(-1)
    fft(2, 0, half)
    relay(3, 2)
    fft(2, half, LOCAL)
    scatter(2)
    relay(3, 3)
    forward(2, 0)
    forward(2, 1)
    relay(2, 0)
    halo_wait(-2)
    fft(1, 0, half)
    forward(2, 2)
    relay(2, 1)
    fft(1, half, LOCAL)
    scatter(1)
    forward(2, 3)
    relay(2, 2)
    forward(1, 0)
    relay(2, 3)
    halo_wait(-3)
    fft(0, 0, half)
    forward(1, 1)
    relay(1, 0)
    fft(0, half, LOCAL)
    scatter(0)
    forward(1, 2)
    relay(1, 1)
    near_wait(3)
    products((mine3, left3, right3), first=True)
    forward(1, 3)
    relay(1, 2)
    beams((3, 2), 0)
    forward(0, 0)
    relay(1, 3)
    beams((3, 2), 1)
    forward(0, 1)
    relay(0, 0)
    far_wait(3)
    near_wait(2)
    products((far3, mine2, left2, right2))
    forward(0, 2)
    relay(0, 1)
    far_wait(2)
    near_wait(1)
    products((far2, mine1, left1, right1))
    forward(0, 3)
    relay(0, 2)
    beams((1, 0), 0)
    relay(0, 3)
    beams((1, 0), 1)
    far_wait(1)
    near_wait(0)
    products((far1, mine0, left0, right0))
    far_wait(0)
    products((far0,), last=True)

    for t in (-1, -2, -3):
        halo(t).wait_send()
    for frame in range(FRAMES):
        for dx in range(NX):
            for copy in (to_right, to_left, onward):
                copy(frame, dx).wait_send()
            sent = send_ref.at[frame, pl.ds(0, XBLOCK - 1 if dx == 0 else XBLOCK)]
            pltpu.make_async_copy(sent, sent, out_sem.at[frame, dx]).wait()


def shards(voltages, coefficients, tile_order, steer_table, beam_index):
    vmem = pl.BlockSpec(memory_space=pltpu.VMEM)
    smem = pl.BlockSpec(memory_space=pltpu.SMEM)
    visibility, beam_power = pl.pallas_call(
        correlator_kernel,
        out_shape=(
            jax.ShapeDtypeStruct((1, ITEMS, 2, TB, TB), jnp.float32),
            jax.ShapeDtypeStruct((2, FRAMES, AVG, NBEAM), jnp.float32),
        ),
        in_specs=[vmem, vmem, vmem, vmem, vmem, smem, vmem, vmem],
        out_specs=(vmem, vmem),
        scratch_shapes=[
            pltpu.VMEM((TAPS - 1, 2, LOCAL, NA, NL), jnp.bfloat16),
            pltpu.VMEM((TAPS * NA, NL), jnp.float32),
            pltpu.VMEM((NCHAN * LOCAL, NL), jnp.float32),
            pltpu.VMEM((FRAMES, NCHAN, LOCAL, NL), jnp.bfloat16),
        ]
        + [pltpu.VMEM((NCHAN, LOCAL, NL), jnp.bfloat16)] * (4 * FRAMES)
        + [
            pltpu.VMEM((ITEMS, 2 * TB, TB), jnp.float32),
            pltpu.VMEM((2, 2 * NBEAM, INPUTS), jnp.bfloat16),
            pltpu.SemaphoreType.DMA((TAPS - 1,)),
            pltpu.SemaphoreType.DMA((TAPS - 1,)),
            pltpu.SemaphoreType.DMA((FRAMES, NX)),
            pltpu.SemaphoreType.DMA((FRAMES, NX)),
            pltpu.SemaphoreType.DMA((FRAMES, NX, 3)),
            pltpu.SemaphoreType.DMA((FRAMES, NX, 3)),
        ],
        compiler_params=pltpu.CompilerParams(
            collective_id=0, has_side_effects=True, vmem_limit_bytes=48 * 1024 * 1024
        ),
        name="correlator",
    )(
        voltages.reshape(2, LOCAL, FRAMES, NA, NL),
        coefficients,
        *tables(),
        tile_order,
        steer_table.reshape(NBEAM, 2 * STATIONS),
        beam_index.reshape(1, NBEAM),
    )
    return visibility, jnp.transpose(beam_power, (0, 3, 1, 2))


def solution(mesh):
    placed = (P(None, "chan", "section", None), P(), P("chan", None), P(), P(None, "chan"))
    return jax.shard_map(
        shards,
        mesh=mesh,
        in_specs=placed,
        out_specs=(P("chan", "section", None, None, None), P(None, None, "section", "chan")),
        check_vma=False,
    )
```

time: 75.7 us -> 81.4 us (1.075)
  Pallas kernels: 70 us -> 76.3 us
    pallas_call x1, Pallas kernels: 70 us -> 76.3 us  [shards(): pl.pallas_call(correlator_kernel, out_shape=(jax.ShapeDtypeStruct((1, ITE...]
where the time goes in v3:
time: 81.4 us; the launch traced here: 81.3 us
  Pallas kernels  76.3 us (94%)
  local copies, waits for them, and re-layouts  4.24 us (5%)
    pallas_call x1, Pallas kernels, shards(): pl.pallas_call(correlator_kernel, out_shape=(jax.ShapeDtypeStruct((1, ITE...  76.3 us
    unnamed x17, local copies, waits for them, and re-layouts  3.14 us

profile of v3, /device:TPU:1, one launch (start us, length us, event | category | flops | bytes accessed | tf_op | source)
XLA Modules:
  0.0 81.3 jit_solution(10303472456140090573)
XLA Ops:
  0.6 0.0 copy-start.6
  0.6 1.2 %copy.10 = bf16[32,8,2,512]{3,1,2,0:T(8,128)(2,1)S(1)} copy(bf16[32,8,2,512]{3,2,1,0:T(2,128)(2,1)} %bitcast.7) | data formatting | bytes 1048576
  1.8 0.0 copy-start
  1.9 0.0 copy-start.1
  1.9 0.0 copy-start.2
  1.9 0.0 copy-start.3
  1.9 0.0 copy-start.4
  1.9 0.0 copy-start.5
  1.9 0.1 copy-done.6
  2.0 1.1 %reshape.13.own_ref = bf16[2,16,4,32,128]{4,3,2,1,0:T(8,128)(2,1)S(1)} reshape(bf16[2,16,4,4096]{3,2,1,0:T(4,128)(2,1)S(1)} %copy-done.6) | data formatting | bytes 2097152 | tf_op jit(solution)/shard_map/reshape | solution.py:416
  3.1 0.0 copy-done
  3.1 0.0 copy-done.1
  3.1 0.0 copy-done.2
  3.2 0.0 copy-done.3
  3.2 0.0 copy-done.4
  3.2 0.0 copy-done.5
  3.2 76.3 %correlator.1 = (f32[1,9,2,128,128]{4,3,2,1,0:T(8,128)S(1)}, f32[2,4,64,256]{3,2,1,0:T(8,128)S(1)}) custom-call(bf16[2,16,4,32,128]{4,3,2,1,0:T(8,128)(2,1)S(1)} %reshape.13.own_ref, f32[4,4096]{1,0:T(4,128)S(1)} %copy-done.1, bf16[64,192]{1,0:T(8,128)(2,1)S(1)} %copy-done.3, f32[2,64,128]{2,1,0:T(8,128)S(1)} %copy-done.2, bf16[64,768]{1,0:T(8,128)(2,1)S(1)} %copy-done, ...), custom_call_target="tpu_custom_call" | custom-call | tf_op jit(solution)/shard_map/correlator/pallas_call | solution.py:386
  79.5 1.0 %copy.13 = f32[1,9,2,128,128]{4,3,2,1,0:T(8,128)} copy(f32[1,9,2,128,128]{4,3,2,1,0:T(8,128)S(1)} %get-tuple-element.8) | data formatting | bytes 2359296
  80.5 0.8 copy.14
Async XLA Ops:
  0.6 1.4 %copy-start.6 = (bf16[2,16,4,4096]{3,2,1,0:T(4,128)(2,1)S(1)}, bf16[2,16,4,4096]{3,2,1,0:T(4,128)(2,1)}, u32[]{:S(2)}) copy-start(bf16[2,16,4,4096]{3,2,1,0:T(4,128)(2,1)} %param.8) | copy-start | bytes 3145732
  1.8 1.3 %copy-start = (bf16[64,768]{1,0:T(8,128)(2,1)S(1)}, bf16[64,768]{1,0:T(8,128)(2,1)}, u32[]{:S(2)}) copy-start(bf16[64,768]{1,0:T(8,128)(2,1)} %constant.8.clone.second_ref) | copy-start | bytes 294916
  1.9 1.3 %copy-start.1 = (f32[4,4096]{1,0:T(4,128)S(1)}, f32[4,4096]{1,0:T(4,128)}, u32[]{:S(2)}) copy-start(f32[4,4096]{1,0:T(4,128)} %coefs_ref.1) | copy-start | bytes 196612
  1.9 1.3 %copy-start.2 = (f32[2,64,128]{2,1,0:T(8,128)S(1)}, f32[2,64,128]{2,1,0:T(8,128)}, u32[]{:S(2)}) copy-start(f32[2,64,128]{2,1,0:T(8,128)} %constant.7.clone.twid_ref) | copy-start | bytes 196612
  1.9 1.3 %copy-start.3 = (bf16[64,192]{1,0:T(8,128)(2,1)S(1)}, bf16[64,192]{1,0:T(8,128)(2,1)}, u32[]{:S(2)}) copy-start(bf16[64,192]{1,0:T(8,128)(2,1)} %constant.6.clone.first_ref) | copy-start | bytes 73732
  1.9 1.3 %copy-start.4 = (s32[256,1]{0,1:T(1,128)S(1)}, s32[256,1]{0,1:T(1,128)}, u32[]{:S(2)}) copy-start(s32[256,1]{0,1:T(1,128)} %param.12) | copy-start | bytes 3076
  1.9 1.3 %copy-start.5 = (s32[1,36]{1,0:T(1,128)S(1)}, s32[1,36]{1,0:T(1,128)}, u32[]{:S(2)}) copy-start(s32[1,36]{1,0:T(1,128)} %order_ref.1) | copy-start | bytes 436

commit v4 on v3

--- a/solution.py
+++ b/solution.py
@@ -9,6 +9,8 @@
 
 NSEC = 4
 FRAMES = 4
+CHUNKS = (3, 2, 4, 1)
+HALOS = (-1, 4, -2)
 NX, NZ, NCORE = 4, 8, 2
 NCHAN = NX * NZ * NCORE
 XBLOCK = NZ * NCORE
@@ -20,7 +22,7 @@
 AVG = 64
 TB = 128
 ITEMS = 9
-UNROLL = 4
+UNROLL = 8
 NBEAM = 256
 STATIONS = 512
 INPUTS = 1024
@@ -29,7 +31,7 @@
 NN = (((1,), (0,)), ((), ()))
 TN = (((0,), (0,)), ((), ()))
 MESH = pl.DeviceIdType.MESH
-BY_RIGHT = ((0, 1), (0, 3))
+BY_RIGHT = ((1, 1), (1, 3), (2, 1), (2, 3), (4, 1), (4, 3))
 
 
 def split_np(table):
@@ -106,6 +108,17 @@
             rows_ref[pl.ds(start + u, NCHAN, stride=LOCAL), :] = section_two[
                 :, u * NL : (u + 1) * NL
             ]
+
+
+def relayout(volts_ref, own_ref, spread_ref):
+    @pl.loop(0, 2 * LOCAL, step=2)
+    def _(n):
+        for u in range(2):
+            q, i = lax.div(n, LOCAL), lax.rem(n, LOCAL) + u
+            samples = volts_ref[q, i].astype(jnp.float32)
+            for a in range(NA):
+                spread_ref[u, pl.ds(a, FRAMES, stride=NA), :] = samples[:, a * NL : (a + 1) * NL]
+            own_ref[q, i] = spread_ref[u].reshape(FRAMES, NA, NL).astype(jnp.bfloat16)
 
 
 def tile(buffer, index):
@@ -144,7 +157,10 @@
         lax.broadcasted_iota(jnp.int32, (NBEAM, NBEAM), 0) == index_ref[...]
     ).astype(jnp.float32).astype(jnp.bfloat16)
     chosen = lax.dot_general(
-        picked, table_ref[...], TN, preferred_element_type=jnp.float32
+        picked,
+        jnp.concatenate([table_ref[:, 0, :], table_ref[:, 1, :]], axis=1),
+        TN,
+        preferred_element_type=jnp.float32,
     ).astype(jnp.bfloat16)
     spread = (
         lax.broadcasted_iota(jnp.int32, (STATIONS, INPUTS), 1)
@@ -157,8 +173,8 @@
         ).astype(jnp.bfloat16)
 
 
-def form_beams(frames, l, mine, weight_ref, beam_ref):
-    spectra = jnp.concatenate([mine[frame][...].reshape(INPUTS, NL) for frame in frames], axis=1)
+def form_beams(frames, l, sources, weight_ref, beam_ref):
+    spectra = jnp.concatenate([sources[frame][...].reshape(INPUTS, NL) for frame in frames], axis=1)
     sums = lax.dot_general(weight_ref[l], spectra, NN, preferred_element_type=jnp.float32)
     for n, frame in enumerate(frames):
         straight = sums[:NBEAM, n * NL : (n + 1) * NL]
@@ -170,20 +186,35 @@
 
 
 def correlator_kernel(
-    own_ref, coefs_ref, first_ref, twid_ref, second_ref, order_ref, table_ref, index_ref,
+    volts_hbm, coefs_hbm, first_hbm, twid_hbm, second_hbm, order_hbm, table_hbm, index_hbm,
     vis_ref, beam_ref,
-    past_ref, coef_ref, rows_ref, send_ref,
-    mine0, mine1, mine2, mine3, left0, left1, left2, left3,
-    right0, right1, right2, right3, far0, far1, far2, far3,
+    volts_ref, coefs_ref, first_ref, twid_ref, second_ref, order_ref, table_ref, index_ref,
+    own_ref, spread_ref, past_ref, next_ref, coef_ref, rows_ref, send_ref,
+    mine1, mine2, mine3, mine4, left1, left2, left3, left4,
+    right1, right2, right3, right4, far1, far2, far3, far4,
     acc_ref, weight_ref,
-    past_send, past_recv, out_sem, in_sem, ysend_sem, yin_sem,
+    load_sem, halo_send, halo_recv, out_sem, in_sem, ysend_sem, yin_sem,
 ):
     section = lax.axis_index("section")
     chan = lax.axis_index("chan")
     x, z, core = chan // XBLOCK, (chan % XBLOCK) // NCORE, chan % NCORE
     right, left = (section + 1) % NSEC, (section + NSEC - 1) % NSEC
-    mine, lefts = (mine0, mine1, mine2, mine3), (left0, left1, left2, left3)
-    rights, fars = (right0, right1, right2, right3), (far0, far1, far2, far3)
+    mine = {1: mine1, 2: mine2, 3: mine3, 4: mine4}
+    lefts = {1: left1, 2: left2, 3: left3, 4: left4}
+    rights = {1: right1, 2: right2, 3: right3, 4: right4}
+    fars = {1: far1, 2: far2, 3: far3, 4: far4}
+
+    arrays = (
+        (volts_hbm, volts_ref), (coefs_hbm, coefs_ref), (first_hbm, first_ref),
+        (twid_hbm, twid_ref), (second_hbm, second_ref), (order_hbm, order_ref),
+        (table_hbm, table_ref), (index_hbm, index_ref),
+    )
+    loads = [
+        pltpu.make_async_copy(source, target, load_sem.at[n])
+        for n, (source, target) in enumerate(arrays)
+    ]
+    for load in loads:
+        load.start()
 
     barrier = pltpu.get_barrier_semaphore()
 
@@ -196,64 +227,78 @@
     for other in (left, right):
         pl.semaphore_signal(barrier, inc=1, device_id=(other, chan), device_id_type=MESH)
 
-    for a in range(NA):
-        coef_ref[pl.ds(a, TAPS, stride=NA), :] = coefs_ref[:, a * NL : (a + 1) * NL]
-
     def sources(q, i, t):
-        return own_ref[q, i, t] if t >= 0 else past_ref[t + TAPS - 1, q, i]
-
-    def fft(frame, lower, upper):
+        if t < 0:
+            return past_ref[t + 2, q, i]
+        return own_ref[q, i, t] if t < FRAMES else next_ref[q, i]
+
+    def spread_coefficients():
+        keep = jnp.where(section < NSEC - 1, 1.0, 0.0)
+        for a in range(NA):
+            coef_ref[0, pl.ds(a, TAPS, stride=NA), :] = coefs_ref[:, a * NL : (a + 1) * NL]
+        coef_ref[1, :NA] = coef_ref[0, :NA]
+        coef_ref[1, NA:] = coef_ref[0, NA:] * keep
+
+    def fft(frame):
         transform(
-            frame, lower, upper, sources, coef_ref, first_ref, twid_ref, second_ref, rows_ref
+            frame, 0, LOCAL, sources, coef_ref.at[1 if frame == FRAMES else 0],
+            first_ref, twid_ref, second_ref, rows_ref,
         )
 
     def halo(t):
+        if t == FRAMES:
+            source, target, peer = own_ref.at[:, :, 0], next_ref, left
+        else:
+            source, target, peer = own_ref.at[:, :, t + FRAMES], past_ref.at[t + 2], right
         return pltpu.make_async_remote_copy(
-            src_ref=own_ref.at[:, :, t + FRAMES],
-            dst_ref=past_ref.at[t + TAPS - 1],
-            send_sem=past_send.at[t + TAPS - 1],
-            recv_sem=past_recv.at[t + TAPS - 1],
-            device_id=(right, chan),
+            src_ref=source,
+            dst_ref=target,
+            send_sem=halo_send.at[HALOS.index(t)],
+            recv_sem=halo_recv.at[HALOS.index(t)],
+            device_id=(peer, chan),
             device_id_type=MESH,
         )
 
     def halo_wait(t):
         halo(t).wait_recv()
-
-        @pl.when(section == 0)
-        def _():
-            past_ref[t + TAPS - 1] = jnp.zeros(past_ref.shape[1:], jnp.bfloat16)
+        if t < 0:
+
+            @pl.when(section == 0)
+            def _():
+                past_ref[t + 2] = jnp.zeros(past_ref.shape[1:], jnp.bfloat16)
 
     def piece(frame, dx, j):
-        dz, dc = j // NCORE, j % NCORE
-        peer = ((x + dx) % NX) * XBLOCK + ((z + dz) % NZ) * NCORE + (core + dc) % NCORE
+        dz, dc = lax.div(j, NCORE), lax.rem(j, NCORE)
+        peer = (
+            lax.rem(x + dx, NX) * XBLOCK + lax.rem(z + dz, NZ) * NCORE + lax.rem(core + dc, NCORE)
+        )
         return pltpu.make_async_remote_copy(
-            src_ref=send_ref.at[frame, peer],
+            src_ref=send_ref.at[frame - 1, peer],
             dst_ref=mine[frame].at[chan],
-            send_sem=out_sem.at[frame, dx],
-            recv_sem=in_sem.at[frame, dx],
+            send_sem=out_sem.at[frame - 1, dx],
+            recv_sem=in_sem.at[frame - 1, dx],
             device_id=(section, peer),
             device_id_type=MESH,
         )
 
-    def scatter(frame):
-        send_ref[frame] = rows_ref[...].astype(jnp.bfloat16).reshape(NCHAN, LOCAL, NL)
+    def ready(frame):
+        send_ref[frame - 1] = rows_ref[...].astype(jnp.bfloat16).reshape(NCHAN, LOCAL, NL)
         pltpu.make_async_copy(
-            send_ref.at[frame, chan], mine[frame].at[chan], in_sem.at[frame, 0]
+            send_ref.at[frame - 1, chan], mine[frame].at[chan], in_sem.at[frame - 1, 0]
         ).start()
-        for dx in range(NX):
-
-            @pl.loop(1 if dx == 0 else 0, XBLOCK)
-            def _(j):
-                piece(frame, dx, j).start()
+
+    def scatter(frame, dx):
+        @pl.loop(1 if dx == 0 else 0, XBLOCK)
+        def _(j):
+            piece(frame, dx, j).start()
 
     def ycopy(source, target, dx, peer, frame, slot):
         part = pl.ds(((x + NX - dx) % NX) * XBLOCK, XBLOCK)
         return pltpu.make_async_remote_copy(
             src_ref=source[frame].at[part],
             dst_ref=target[frame].at[part],
-            send_sem=ysend_sem.at[frame, dx, slot],
-            recv_sem=yin_sem.at[frame, dx, slot],
+            send_sem=ysend_sem.at[frame - 1, dx, slot],
+            recv_sem=yin_sem.at[frame - 1, dx, slot],
             device_id=(peer, chan),
             device_id_type=MESH,
         )
@@ -271,7 +316,7 @@
 
     def forward(frame, dx):
         part = mine[frame].at[pl.ds(((x + NX - dx) % NX) * XBLOCK, XBLOCK)]
-        pltpu.make_async_copy(part, part, in_sem.at[frame, dx]).wait()
+        pltpu.make_async_copy(part, part, in_sem.at[frame - 1, dx]).wait()
         to_left(frame, dx).start()
         to_right(frame, dx).start()
 
@@ -288,8 +333,7 @@
             onward(frame, dx).wait_recv()
 
     def products(buffers, first=False, last=False):
-        @pl.loop(0, ITEMS)
-        def _(item):
+        for item in range(ITEMS):
             multiply(
                 item, buffers, acc_ref, vis_ref, order_ref, section * ITEMS, first, last
             )
@@ -298,102 +342,131 @@
         make_weights(l, table_ref, index_ref, weight_ref)
 
     def beams(frames, l):
-        form_beams(frames, l, mine, weight_ref, beam_ref)
-
-    half = LOCAL // 2
-    fft(3, 0, LOCAL)
+        form_beams(frames, l, {**mine, 0: left4}, weight_ref, beam_ref)
+
+    loads[0].wait()
+    relayout(volts_ref, own_ref, spread_ref)
+    for load in loads[1:]:
+        load.wait()
+    spread_coefficients()
     pl.semaphore_wait(barrier, NCHAN + 1)
-    for t in (-1, -2, -3):
+    for t in (-1, FRAMES, -2):
         halo(t).start()
-    scatter(3)
+    fft(3)
+    ready(3)
+    scatter(3, 0)
+    scatter(3, 1)
+    scatter(3, 2)
+    scatter(3, 3)
     forward(3, 0)
+    forward(3, 1)
+    forward(3, 2)
+    forward(3, 3)
+    halo_wait(-1)
+    fft(2)
+    ready(2)
+    scatter(2, 0)
+    scatter(2, 1)
+    relay(3, 0)
+    scatter(2, 2)
+    scatter(2, 3)
+    relay(3, 1)
+    halo_wait(FRAMES)
+    fft(4)
+    ready(4)
+    forward(2, 0)
+    relay(3, 2)
+    scatter(4, 0)
+    forward(2, 1)
+    scatter(4, 1)
+    relay(3, 3)
+    forward(2, 2)
+    scatter(4, 2)
+    scatter(4, 3)
+    forward(2, 3)
+    halo_wait(-2)
+    fft(1)
+    ready(1)
+    forward(4, 0)
+    scatter(1, 0)
+    scatter(1, 1)
+    forward(4, 1)
+    relay(2, 0)
+    scatter(1, 2)
+    scatter(1, 3)
+    forward(4, 2)
+    relay(2, 1)
+    forward(4, 3)
     weights(0)
-    forward(3, 1)
+    forward(1, 0)
+    relay(2, 2)
     weights(1)
-    forward(3, 2)
-    relay(3, 0)
-    forward(3, 3)
-    relay(3, 1)
-    halo_wait(-1)
-    fft(2, 0, half)
-    relay(3, 2)
-    fft(2, half, LOCAL)
-    scatter(2)
-    relay(3, 3)
-    forward(2, 0)
-    forward(2, 1)
-    relay(2, 0)
-    halo_wait(-2)
-    fft(1, 0, half)
-    forward(2, 2)
-    relay(2, 1)
-    fft(1, half, LOCAL)
-    scatter(1)
-    forward(2, 3)
-    relay(2, 2)
-    forward(1, 0)
+    forward(1, 1)
     relay(2, 3)
-    halo_wait(-3)
-    fft(0, 0, half)
-    forward(1, 1)
-    relay(1, 0)
-    fft(0, half, LOCAL)
-    scatter(0)
     forward(1, 2)
-    relay(1, 1)
+    relay(4, 0)
+    forward(1, 3)
+    relay(4, 1)
     near_wait(3)
     products((mine3, left3, right3), first=True)
-    forward(1, 3)
-    relay(1, 2)
+    relay(4, 2)
     beams((3, 2), 0)
-    forward(0, 0)
-    relay(1, 3)
+    relay(4, 3)
     beams((3, 2), 1)
-    forward(0, 1)
-    relay(0, 0)
     far_wait(3)
     near_wait(2)
     products((far3, mine2, left2, right2))
-    forward(0, 2)
-    relay(0, 1)
+    relay(1, 0)
+    near_wait(4)
+    beams((1, 0), 0)
+    relay(1, 1)
+    beams((1, 0), 1)
+    relay(1, 2)
     far_wait(2)
+    products((far2, mine4, left4, right4))
+    relay(1, 3)
+    far_wait(4)
     near_wait(1)
-    products((far2, mine1, left1, right1))
-    forward(0, 3)
-    relay(0, 2)
-    beams((1, 0), 0)
-    relay(0, 3)
-    beams((1, 0), 1)
+    products((far4, mine1, left1, right1))
     far_wait(1)
-    near_wait(0)
-    products((far1, mine0, left0, right0))
-    far_wait(0)
-    products((far0,), last=True)
-
-    for t in (-1, -2, -3):
+    products((far1,), last=True)
+
+    for t in (-1, FRAMES, -2):
         halo(t).wait_send()
-    for frame in range(FRAMES):
+    for frame in CHUNKS:
         for dx in range(NX):
             for copy in (to_right, to_left, onward):
                 copy(frame, dx).wait_send()
-            sent = send_ref.at[frame, pl.ds(0, XBLOCK - 1 if dx == 0 else XBLOCK)]
-            pltpu.make_async_copy(sent, sent, out_sem.at[frame, dx]).wait()
+            sent = send_ref.at[frame - 1, pl.ds(0, XBLOCK - 1 if dx == 0 else XBLOCK)]
+            pltpu.make_async_copy(sent, sent, out_sem.at[frame - 1, dx]).wait()
 
 
 def shards(voltages, coefficients, tile_order, steer_table, beam_index):
     vmem = pl.BlockSpec(memory_space=pltpu.VMEM)
-    smem = pl.BlockSpec(memory_space=pltpu.SMEM)
+    hbm = pl.BlockSpec(memory_space=pltpu.HBM)
+    first, twiddle, second = tables()
     visibility, beam_power = pl.pallas_call(
         correlator_kernel,
         out_shape=(
-            jax.ShapeDtypeStruct((1, ITEMS, 2, TB, TB), jnp.float32),
-            jax.ShapeDtypeStruct((2, FRAMES, AVG, NBEAM), jnp.float32),
+            pltpu.VMEM((1, ITEMS, 2, TB, TB), jnp.float32),
+            pltpu.VMEM((2, FRAMES, AVG, NBEAM), jnp.float32),
         ),
-        in_specs=[vmem, vmem, vmem, vmem, vmem, smem, vmem, vmem],
+        in_specs=[hbm] * 8,
         out_specs=(vmem, vmem),
         scratch_shapes=[
-            pltpu.VMEM((TAPS - 1, 2, LOCAL, NA, NL), jnp.bfloat16),
-            pltpu.VMEM((TAPS * NA, NL), jnp.float32),
+            pltpu.VMEM(voltages.shape, voltages.dtype),
+            pltpu.VMEM(coefficients.shape, coefficients.dtype),
+            pltpu.VMEM(first.shape, first.dtype),
+            pltpu.VMEM(twiddle.shape, twiddle.dtype),
+            pltpu.VMEM(second.shape, second.dtype),
+            pltpu.SMEM(tile_order.shape, tile_order.dtype),
+            pltpu.VMEM(steer_table.shape, steer_table.dtype),
+            pltpu.VMEM((1, NBEAM), beam_index.dtype),
+            pltpu.VMEM((2, LOCAL, FRAMES, NA, NL), jnp.bfloat16),
+            pltpu.VMEM((2, FRAMES * NA, NL), jnp.float32),
+            pltpu.VMEM((2, 2, LOCAL, NA, NL), jnp.bfloat16),
+            pltpu.VMEM((2, LOCAL, NA, NL), jnp.bfloat16),
+            pltpu.VMEM((2, TAPS * NA, NL), jnp.float32),
             pltpu.VMEM((NCHAN * LOCAL, NL), jnp.float32),
             pltpu.VMEM((FRAMES, NCHAN, LOCAL, NL), jnp.bfloat16),
         ]
@@ -401,23 +474,26 @@
         + [
             pltpu.VMEM((ITEMS, 2 * TB, TB), jnp.float32),
             pltpu.VMEM((2, 2 * NBEAM, INPUTS), jnp.bfloat16),
-            pltpu.SemaphoreType.DMA((TAPS - 1,)),
-            pltpu.SemaphoreType.DMA((TAPS - 1,)),
+            pltpu.SemaphoreType.DMA((8,)),
+            pltpu.SemaphoreType.DMA((3,)),
+            pltpu.SemaphoreType.DMA((3,)),
             pltpu.SemaphoreType.DMA((FRAMES, NX)),
             pltpu.SemaphoreType.DMA((FRAMES, NX)),
             pltpu.SemaphoreType.DMA((FRAMES, NX, 3)),
             pltpu.SemaphoreType.DMA((FRAMES, NX, 3)),
         ],
         compiler_params=pltpu.CompilerParams(
-            collective_id=0, has_side_effects=True, vmem_limit_bytes=48 * 1024 * 1024
+            collective_id=0, has_side_effects=True
         ),
         name="correlator",
     )(
-        voltages.reshape(2, LOCAL, FRAMES, NA, NL),
+        voltages,
         coefficients,
-        *tables(),
+        first,
+        twiddle,
+        second,
         tile_order,
-        steer_table.reshape(NBEAM, 2 * STATIONS),
+        steer_table,
         beam_index.reshape(1, NBEAM),
     )
     return visibility, jnp.transpose(beam_power, (0, 3, 1, 2))

time: 81.4 us -> 65.3 us (0.80)
  Pallas kernels: 76.3 us -> 62.7 us
  local copies, waits for them, and re-layouts: 4.24 us -> 1.81 us
    pallas_call x1, Pallas kernels: 76.3 us -> 62.7 us  [shards(): pl.pallas_call(correlator_kernel, out_shape=(pltpu.VMEM((1, ITEMS, 2, TB,...]
    unnamed x17 -> x2, local copies, waits for them, and re-layouts: 3.14 us -> 1.81 us
    reshape x1 -> x0, local copies, waits for them, and re-layouts: 1.1 us -> none  [shards(): voltages.reshape(2, LOCAL, FRAMES, NA, NL)]
where the time goes in v4:
time: 65.3 us; the launch traced here: 65.2 us
  Pallas kernels  62.7 us (96%)
  local copies, waits for them, and re-layouts  1.81 us (3%)
    pallas_call x1, Pallas kernels, shards(): pl.pallas_call(correlator_kernel, out_shape=(pltpu.VMEM((1, ITEMS, 2, TB,...  62.7 us
    unnamed x2, local copies, waits for them, and re-layouts  1.81 us

profile of v4, /device:TPU:1, one launch (start us, length us, event | category | flops | bytes accessed | tf_op | source)
XLA Modules:
  0.0 65.2 jit_solution(8176657270749697780)
XLA Ops:
  0.6 62.7 %correlator.1 = (f32[1,9,2,128,128]{4,3,2,1,0:T(8,128)S(1)}, f32[2,4,64,256]{3,2,1,0:T(8,128)S(1)}) custom-call(bf16[2,16,4,4096]{3,2,1,0:T(4,128)(2,1)} %volts_hbm.1, f32[4,4096]{1,0:T(4,128)} %coefs_hbm.1, bf16[64,192]{1,0:T(8,128)(2,1)} %constant.6.clone.first_hbm, f32[2,64,128]{2,1,0:T(8,128)} %constant.7.clone.twid_hbm, ...), custom_call_target="tpu_custom_call" | custom-call | tf_op jit(solution)/shard_map/correlator/pallas_call | solution.py:448
  63.4 1.0 %copy.12 = f32[1,9,2,128,128]{4,3,2,1,0:T(8,128)} copy(f32[1,9,2,128,128]{4,3,2,1,0:T(8,128)S(1)} %get-tuple-element.6) | data formatting | bytes 2359296
  64.4 0.8 %copy.13 = f32[2,256,4,64]{1,3,2,0:T(8,128)} copy(f32[2,256,4,64]{1,3,2,0:T(8,128)S(1)} %bitcast.2) | data formatting | bytes 1048576

commit v5 on v4

--- a/solution.py
+++ b/solution.py
@@ -22,7 +22,8 @@
 AVG = 64
 TB = 128
 ITEMS = 9
-UNROLL = 8
+UNROLL = 16
+ZORDER = (4, 3, 5, 2, 6, 1, 7, 0)
 NBEAM = 256
 STATIONS = 512
 INPUTS = 1024
@@ -93,11 +94,13 @@
             real = jnp.concatenate([real, real], axis=0)
             imag = jnp.concatenate([imag, imag], axis=0)
             real, imag = real * cosine + imag * sine, imag * cosine - real * sine
-            rows = jnp.concatenate(
-                [jnp.concatenate([real, imag], axis=1), jnp.concatenate([imag, -real], axis=1)], axis=0
-            )
-            high, low = split(rows)
-            turned.append(jnp.concatenate([high, high, low], axis=1))
+            parts = [
+                jnp.concatenate(
+                    [jnp.concatenate([re, im], axis=1), jnp.concatenate([im, -re], axis=1)], axis=0
+                )
+                for re, im in zip(split(real), split(imag))
+            ]
+            turned.append(jnp.concatenate([parts[0], parts[0], parts[1]], axis=1))
         section_two = lax.dot_general(
             second_ref[...],
             jnp.concatenate(turned, axis=0),
@@ -111,9 +114,9 @@
 
 
 def relayout(volts_ref, own_ref, spread_ref):
-    @pl.loop(0, 2 * LOCAL, step=2)
+    @pl.loop(0, 2 * LOCAL, step=8)
     def _(n):
-        for u in range(2):
+        for u in range(8):
             q, i = lax.div(n, LOCAL), lax.rem(n, LOCAL) + u
             samples = volts_ref[q, i].astype(jnp.float32)
             for a in range(NA):
@@ -267,8 +270,7 @@
             def _():
                 past_ref[t + 2] = jnp.zeros(past_ref.shape[1:], jnp.bfloat16)
 
-    def piece(frame, dx, j):
-        dz, dc = lax.div(j, NCORE), lax.rem(j, NCORE)
+    def piece(frame, dx, dz, dc):
         peer = (
             lax.rem(x + dx, NX) * XBLOCK + lax.rem(z + dz, NZ) * NCORE + lax.rem(core + dc, NCORE)
         )
@@ -288,9 +290,10 @@
         ).start()
 
     def scatter(frame, dx):
-        @pl.loop(1 if dx == 0 else 0, XBLOCK)
-        def _(j):
-            piece(frame, dx, j).start()
+        for dz in ZORDER:
+            for dc in range(NCORE):
+                if (dx, dz, dc) != (0, 0, 0):
+                    piece(frame, dx, dz, dc).start()
 
     def ycopy(source, target, dx, peer, frame, slot):
         part = pl.ds(((x + NX - dx) % NX) * XBLOCK, XBLOCK)
@@ -367,46 +370,46 @@
     ready(2)
     scatter(2, 0)
     scatter(2, 1)
-    relay(3, 0)
     scatter(2, 2)
     scatter(2, 3)
+    relay(3, 0)
     relay(3, 1)
     halo_wait(FRAMES)
     fft(4)
     ready(4)
-    forward(2, 0)
-    relay(3, 2)
     scatter(4, 0)
-    forward(2, 1)
     scatter(4, 1)
-    relay(3, 3)
-    forward(2, 2)
     scatter(4, 2)
     scatter(4, 3)
-    forward(2, 3)
+    relay(3, 2)
+    forward(2, 0)
     halo_wait(-2)
     fft(1)
     ready(1)
-    forward(4, 0)
     scatter(1, 0)
     scatter(1, 1)
-    forward(4, 1)
-    relay(2, 0)
     scatter(1, 2)
     scatter(1, 3)
+    relay(3, 3)
+    forward(2, 1)
+    forward(2, 2)
+    forward(2, 3)
+    relay(2, 0)
+    forward(4, 0)
+    forward(4, 1)
+    relay(2, 1)
     forward(4, 2)
-    relay(2, 1)
     forward(4, 3)
+    relay(2, 2)
     weights(0)
     forward(1, 0)
-    relay(2, 2)
+    relay(2, 3)
     weights(1)
     forward(1, 1)
-    relay(2, 3)
+    relay(4, 0)
     forward(1, 2)
-    relay(4, 0)
+    relay(4, 1)
     forward(1, 3)
-    relay(4, 1)
     near_wait(3)
     products((mine3, left3, right3), first=True)
     relay(4, 2)
@@ -463,7 +466,7 @@
             pltpu.VMEM(steer_table.shape, steer_table.dtype),
             pltpu.VMEM((1, NBEAM), beam_index.dtype),
             pltpu.VMEM((2, LOCAL, FRAMES, NA, NL), jnp.bfloat16),
-            pltpu.VMEM((2, FRAMES * NA, NL), jnp.float32),
+            pltpu.VMEM((8, FRAMES * NA, NL), jnp.float32),
             pltpu.VMEM((2, 2, LOCAL, NA, NL), jnp.bfloat16),
             pltpu.VMEM((2, LOCAL, NA, NL), jnp.bfloat16),
             pltpu.VMEM((2, TAPS * NA, NL), jnp.float32),

time: 65.3 us -> 63.9 us (0.979)
  Pallas kernels: 62.7 us -> 61.3 us
    pallas_call x1, Pallas kernels: 62.7 us -> 61.3 us  [shards(): pl.pallas_call(correlator_kernel, out_shape=(pltpu.VMEM((1, ITEMS, 2, TB,...]
where the time goes in v5:
time: 63.9 us; the launch traced here: 63.8 us
  Pallas kernels  61.3 us (96%)
  local copies, waits for them, and re-layouts  1.81 us (3%)
  between operations  0.64 us (1%)
    pallas_call x1, Pallas kernels, shards(): pl.pallas_call(correlator_kernel, out_shape=(pltpu.VMEM((1, ITEMS, 2, TB,...  61.3 us
    unnamed x2, local copies, waits for them, and re-layouts  1.81 us

profile of v5, /device:TPU:1, one launch (start us, length us, event | category | flops | bytes accessed | tf_op | source)
XLA Modules:
  0.0 63.8 jit_solution(7610555203551000646)
XLA Ops:
  0.6 61.3 %correlator.1 = (f32[1,9,2,128,128]{4,3,2,1,0:T(8,128)S(1)}, f32[2,4,64,256]{3,2,1,0:T(8,128)S(1)}) custom-call(bf16[2,16,4,4096]{3,2,1,0:T(4,128)(2,1)} %volts_hbm.1, f32[4,4096]{1,0:T(4,128)} %coefs_hbm.1, bf16[64,192]{1,0:T(8,128)(2,1)} %constant.6.clone.first_hbm, f32[2,64,128]{2,1,0:T(8,128)} %constant.7.clone.twid_hbm, ...), custom_call_target="tpu_custom_call" | custom-call | tf_op jit(solution)/shard_map/correlator/pallas_call | solution.py:451
  62.0 1.0 %copy.12 = f32[1,9,2,128,128]{4,3,2,1,0:T(8,128)} copy(f32[1,9,2,128,128]{4,3,2,1,0:T(8,128)S(1)} %get-tuple-element.6) | data formatting | bytes 2359296
  63.0 0.8 %copy.13 = f32[2,256,4,64]{1,3,2,0:T(8,128)} copy(f32[2,256,4,64]{1,3,2,0:T(8,128)S(1)} %bitcast.2) | data formatting | bytes 1048576

commit v6 on v5

--- a/solution.py
+++ b/solution.py
@@ -32,7 +32,7 @@
 NN = (((1,), (0,)), ((), ()))
 TN = (((0,), (0,)), ((), ()))
 MESH = pl.DeviceIdType.MESH
-BY_RIGHT = ((1, 1), (1, 3), (2, 1), (2, 3), (4, 1), (4, 3))
+BY_RIGHT = ((1, 1), (1, 3), (2, 3), (4, 1), (4, 3))
 
 
 def split_np(table):
@@ -444,6 +444,17 @@
             pltpu.make_async_copy(sent, sent, out_sem.at[frame - 1, dx]).wait()
 
 
+def store_kernel(vis_ref, beam_ref, vis_hbm, beam_hbm, sems):
+    copies = [
+        pltpu.make_async_copy(vis_ref, vis_hbm, sems.at[0]),
+        pltpu.make_async_copy(beam_ref, beam_hbm, sems.at[1]),
+    ]
+    for copy in copies:
+        copy.start()
+    for copy in copies:
+        copy.wait()
+
+
 def shards(voltages, coefficients, tile_order, steer_table, beam_index):
     vmem = pl.BlockSpec(memory_space=pltpu.VMEM)
     hbm = pl.BlockSpec(memory_space=pltpu.HBM)
@@ -499,6 +510,18 @@
         steer_table,
         beam_index.reshape(1, NBEAM),
     )
+    visibility, beam_power = pl.pallas_call(
+        store_kernel,
+        out_shape=(
+            jax.ShapeDtypeStruct(visibility.shape, visibility.dtype),
+            jax.ShapeDtypeStruct(beam_power.shape, beam_power.dtype),
+        ),
+        in_specs=[vmem, vmem],
+        out_specs=(hbm, hbm),
+        scratch_shapes=[pltpu.SemaphoreType.DMA((2,))],
+        compiler_params=pltpu.CompilerParams(vmem_limit_bytes=4 * 1024 * 1024),
+        name="store",
+    )(visibility, beam_power)
     return visibility, jnp.transpose(beam_power, (0, 3, 1, 2))
 
 

time: 63.9 us -> 63.3 us (level)
  local copies, waits for them, and re-layouts: 1.81 us -> 0 us
  Pallas kernels: 61.3 us -> 62.4 us
    unnamed x2 -> x0, local copies, waits for them, and re-layouts: 1.81 us -> none
    pallas_call x0 -> x1, Pallas kernels: none -> 1.2 us  [shards(): pl.pallas_call(store_kernel, out_shape=(jax.ShapeDtypeStruct(visibility.s...]
where the time goes in v6:
time: 63.3 us; the launch traced here: 63.2 us
  Pallas kernels  62.4 us (99%)
  between operations  0.8 us (1%)
    pallas_call x1, Pallas kernels, shards(): pl.pallas_call(correlator_kernel, out_shape=(pltpu.VMEM((1, ITEMS, 2, TB,...  61.1 us

profile of v6, /device:TPU:1, one launch (start us, length us, event | category | flops | bytes accessed | tf_op | source)
XLA Modules:
  0.0 63.2 jit_solution(1402295054508902628)
XLA Ops:
  0.6 61.1 %correlator.1 = (f32[1,9,2,128,128]{4,3,2,1,0:T(8,128)S(1)}, f32[2,4,64,256]{3,2,1,0:T(8,128)S(1)}) custom-call(bf16[2,16,4,4096]{3,2,1,0:T(4,128)(2,1)} %volts_hbm.1, f32[4,4096]{1,0:T(4,128)} %coefs_hbm.1, bf16[64,192]{1,0:T(8,128)(2,1)} %constant.6.clone.first_hbm, f32[2,64,128]{2,1,0:T(8,128)} %constant.7.clone.twid_hbm, ...), custom_call_target="tpu_custom_call" | custom-call | tf_op jit(solution)/shard_map/correlator/pallas_call | solution.py:462
  61.8 1.2 %store.1 = (f32[1,9,2,128,128]{4,3,2,1,0:T(8,128)}, f32[2,4,64,256]{3,2,1,0:T(8,128)}) custom-call(f32[1,9,2,128,128]{4,3,2,1,0:T(8,128)S(1)} %get-tuple-element.6.vis_ref, f32[2,4,64,256]{3,2,1,0:T(8,128)S(1)} %get-tuple-element.7.beam_ref), custom_call_target="tpu_custom_call" | custom-call | tf_op jit(solution)/shard_map/store/pallas_call | solution.py:513

commit v7 on v6

--- a/solution.py
+++ b/solution.py
@@ -349,12 +349,12 @@
 
     loads[0].wait()
     relayout(volts_ref, own_ref, spread_ref)
+    pl.semaphore_wait(barrier, NCHAN + 1)
+    for t in (-1, FRAMES, -2):
+        halo(t).start()
     for load in loads[1:]:
         load.wait()
     spread_coefficients()
-    pl.semaphore_wait(barrier, NCHAN + 1)
-    for t in (-1, FRAMES, -2):
-        halo(t).start()
     fft(3)
     ready(3)
     scatter(3, 0)

time: 63.3 us -> 63.3 us (level)
  no operation moved by 1% of the time
where the time goes in v7:
time: 63.3 us; the launch traced here: 63.2 us
  Pallas kernels  62.4 us (99%)
  between operations  0.8 us (1%)
    pallas_call x1, Pallas kernels, shards(): pl.pallas_call(correlator_kernel, out_shape=(pltpu.VMEM((1, ITEMS, 2, TB,...  61.2 us

profile of v7, /device:TPU:1, one launch (start us, length us, event | category | flops | bytes accessed | tf_op | source)
XLA Modules:
  0.0 63.2 jit_solution(1121547626810240205)
XLA Ops:
  0.6 61.2 %correlator.1 = (f32[1,9,2,128,128]{4,3,2,1,0:T(8,128)S(1)}, f32[2,4,64,256]{3,2,1,0:T(8,128)S(1)}) custom-call(bf16[2,16,4,4096]{3,2,1,0:T(4,128)(2,1)} %volts_hbm.1, f32[4,4096]{1,0:T(4,128)} %coefs_hbm.1, bf16[64,192]{1,0:T(8,128)(2,1)} %constant.6.clone.first_hbm, f32[2,64,128]{2,1,0:T(8,128)} %constant.7.clone.twid_hbm, ...), custom_call_target="tpu_custom_call" | custom-call | tf_op jit(solution)/shard_map/correlator/pallas_call | solution.py:462
  61.8 1.2 %store.1 = (f32[1,9,2,128,128]{4,3,2,1,0:T(8,128)}, f32[2,4,64,256]{3,2,1,0:T(8,128)}) custom-call(f32[1,9,2,128,128]{4,3,2,1,0:T(8,128)S(1)} %get-tuple-element.6.vis_ref, f32[2,4,64,256]{3,2,1,0:T(8,128)S(1)} %get-tuple-element.7.beam_ref), custom_call_target="tpu_custom_call" | custom-call | tf_op jit(solution)/shard_map/store/pallas_call | solution.py:513
